TPU v7x, 256 devices: a whole 4x4x8 slice. The times are simulated.
256 devices in a mesh: dp: 4 (over x), expert: 64 (over z, y, core).
Axes of the slice: x: 4, y: 4, z: 8, core: 2. Of those that a mesh axis runs over, the one named last changes fastest.
Arguments:
- cell_table: bfloat16 [524288, 256], P(('dp', 'expert')), may hold values from -6 to 6
- sample_index: int32 [262144], P(('dp', 'expert')), may hold values from 0 to 2047
- region: int32 [262144, 1], P(('dp', 'expert')), may hold values from 0 to 63; in each aligned block of 1024 rows (0 to 1023, 1024 to 2047, ...) at most 32 rows name the same one
- targets: bfloat16 [262144, 256], P(('dp', 'expert')), may hold values from -6 to 6
- trunk_weight: bfloat16 [256, 256], replicated, may hold values from -0.375 to 0.375
- expert_params: float32 [64, 2, 256, 2048], P('expert', None, None, 'dp'), may hold values from -0.375 to 0.375
- first_moment: float32 [64, 2, 256, 2048], P('expert', None, None, 'dp'), may hold values from -4 to 4
- second_moment: float32 [64, 2, 256, 2048], P('expert', None, None, 'dp'), may hold values from 0.05 to 1
Outputs:
- trunk_grad: float32 [256, 256], replicated
- row_loss: float32 [262144], P(('dp', 'expert'))
- new_params: float32 [64, 2, 256, 2048], P('expert', None, None, 'dp')
- new_first: float32 [64, 2, 256, 2048], P('expert', None, None, 'dp')
- new_second: float32 [64, 2, 256, 2048], P('expert', None, None, 'dp')
Inputs may be any that keep to these rules, and one draw needn't show every extreme that they name: In the 1024 rows of one device no region is named more than 32 times; some region exactly 32 times. `sample_index`: indexes the rows of the same device's block of cell_table.
All inputs are finite; a program needn't handle non-finite values.
Results may differ from a plain program's by a relative error of at most 0.0044.
Values may be sent and summed in bfloat16 or wider, within the bound.
A program may use at most 128 MiB of HBM per device.

v0:
```python
import jax
import jax.numpy as jnp
from jax import lax
from jax.sharding import PartitionSpec as P

loss_scale = 1.0 / 32.0
beta_one = 0.9
beta_two = 0.999
learn_rate = 0.05
adam_eps = 1e-08
adam_step = 10


def silu_slope(values):
    sigma = jax.nn.sigmoid(values)
    return sigma * (1.0 + values * (1.0 - sigma))


def expert_forward(arrived, w_up, w_down):
    up_pre = jnp.dot(arrived, w_up, preferred_element_type=jnp.float32)
    hidden = jax.nn.silu(up_pre).astype(jnp.bfloat16)
    predicted = lax.dot_general(
        hidden, w_down, (((1,), (1,)), ((), ())), preferred_element_type=jnp.float32
    )
    return (up_pre, hidden, predicted)


def expert_backward(arrived, up_pre, hidden, scaled_error, w_up, w_down):
    grad_down = lax.dot_general(
        scaled_error, hidden, (((0,), (0,)), ((), ())), preferred_element_type=jnp.float32
    )
    hidden_grad = jnp.dot(scaled_error, w_down, preferred_element_type=jnp.float32)
    pre_grad = (hidden_grad * silu_slope(up_pre)).astype(jnp.bfloat16)
    grad_up = lax.dot_general(
        arrived, pre_grad, (((0,), (0,)), ((), ())), preferred_element_type=jnp.float32
    )
    input_grad = lax.dot_general(
        pre_grad, w_up, (((1,), (1,)), ((), ())), preferred_element_type=jnp.float32
    ).astype(jnp.bfloat16)
    return (grad_up, grad_down, input_grad)


def error_terms(predicted, target):
    errors = predicted - target.astype(jnp.float32)
    losses = jnp.sum(errors * errors, axis=1) * (0.5 * loss_scale)
    return (losses, (errors * loss_scale).astype(jnp.bfloat16))


def adam_update(params, first, second, grads):
    first_new = beta_one * first + (1.0 - beta_one) * grads
    second_new = beta_two * second + (1.0 - beta_two) * grads * grads
    first_hat = first_new / (1.0 - beta_one**adam_step)
    second_hat = second_new / (1.0 - beta_two**adam_step)
    return (
        params - learn_rate * first_hat / (jnp.sqrt(second_hat) + adam_eps),
        first_new,
        second_new,
    )


def on_device(
    cell_table,
    sample_index,
    region,
    targets,
    trunk_weight,
    expert_params,
    first_moment,
    second_moment,
):
    rows = sample_index.shape[0]
    width = cell_table.shape[1]
    experts = lax.axis_size("expert")
    capacity = 2 * rows // experts
    features = jnp.take(cell_table, sample_index, axis=0)
    trunk_pre = jnp.dot(features, trunk_weight, preferred_element_type=jnp.float32)
    trunk_out = (features.astype(jnp.float32) + jax.nn.silu(trunk_pre)).astype(jnp.bfloat16)
    routed = region[:, 0]
    onehot = (routed[:, None] == jnp.arange(experts, dtype=jnp.int32)[None, :]).astype(jnp.int32)
    slots = jnp.sum(jnp.cumsum(onehot, axis=0) * onehot, axis=1) - 1
    places = routed * capacity + slots

    def pack(values):
        empty = jnp.zeros((experts * capacity,) + values.shape[1:], values.dtype)
        return empty.at[places].set(values).reshape((experts, capacity) + values.shape[1:])

    gathered = lax.all_gather(expert_params.astype(jnp.bfloat16), "dp", axis=3, tiled=True)
    w_up = gathered[0, 0]
    w_down = gathered[0, 1]
    arrived = lax.all_to_all(
        pack(trunk_out), "expert", split_axis=0, concat_axis=0, tiled=True
    ).reshape(-1, width)
    up_pre, hidden, predicted = expert_forward(arrived, w_up, w_down)
    returned = lax.all_to_all(
        predicted.reshape(experts, capacity, width),
        "expert",
        split_axis=0,
        concat_axis=0,
        tiled=True,
    )
    row_loss, row_error = error_terms(returned.reshape(-1, width)[places], targets)
    error_there = lax.all_to_all(
        pack(row_error), "expert", split_axis=0, concat_axis=0, tiled=True
    ).reshape(-1, width)
    grad_up, grad_down, input_grad = expert_backward(
        arrived, up_pre, hidden, error_there, w_up, w_down
    )
    back_grad = lax.all_to_all(
        input_grad.reshape(experts, capacity, width),
        "expert",
        split_axis=0,
        concat_axis=0,
        tiled=True,
    )
    row_grad = back_grad.reshape(-1, width)[places]
    trunk_slope = (row_grad.astype(jnp.float32) * silu_slope(trunk_pre)).astype(jnp.bfloat16)
    trunk_local = lax.dot_general(
        features, trunk_slope, (((0,), (0,)), ((), ())), preferred_element_type=jnp.float32
    )
    trunk_grad = lax.psum(trunk_local, ("dp", "expert"))
    grads = jnp.stack([grad_up, grad_down])[None]
    grad_shard = lax.psum_scatter(grads, "dp", scatter_dimension=3, tiled=True)
    new_params, new_first, new_second = adam_update(
        expert_params, first_moment, second_moment, grad_shard
    )
    return (trunk_grad, row_loss, new_params, new_first, new_second)


def solution(mesh):
    placed = (
        P(("dp", "expert"), None),
        P(("dp", "expert")),
        P(("dp", "expert"), None),
        P(("dp", "expert"), None),
        P(),
        P("expert", None, None, "dp"),
        P("expert", None, None, "dp"),
        P("expert", None, None, "dp"),
    )
    return jax.shard_map(
        on_device,
        mesh=mesh,
        in_specs=placed,
        out_specs=(
            P(),
            P(("dp", "expert")),
            P("expert", None, None, "dp"),
            P("expert", None, None, "dp"),
            P("expert", None, None, "dp"),
        ),
        check_vma=False,
    )
```

profile of v0, /device:TPU:1, one launch (start us, length us, event | category | flops | bytes accessed | tf_op | source)
XLA Modules:
  0.0 532.4 jit_solution(5352181415112622577)
XLA Ops:
  7.3 2.2 convert_element_type.38
  9.5 0.7 fusion.15
  10.2 18.0 %reduce-window.6 = s32[64,8,128]{2,1,0:T(8,128)S(1)} reduce-window(s32[64,8,128]{2,1,0:T(8,128)S(1)} %fusion.15, s32[]{:T(128)} %constant.18.clone.1), window={size=1x1x128 pad=0_0x0_0x127_0}, to_apply=%region_0.1 | reduce-window | flops 8323072 | bytes 524292 | tf_op jit(solution)/shard_map/reduce-window
  28.7 0.7 fusion.16
  29.4 3.9 gather_fusion
  33.5 0.4 fusion.18
  33.9 6.0 %scatter_custom_fusion = bf16[2048,256]{1,0:T(8,128)(2,1)S(1)} fusion(s32[1024]{0:T(1024)S(1)} %bitcast.70, bf16[]{:T(256)} %constant.22.clone.1, f32[1024,256]{1,0:T(8,128)S(1)} %fusion.18, f32[]{:T(128)} %constant.15.clone.1, bf16[1024,256]{1,0:T(8,128)(2,1)S(1)} %gather_fusion, pred[1024]{0:T(1024)(128)(4,1)S(1)} %compare_and_fusion), kind=kCustom, calls=%fused_computation.32 | custom fusion | flops 2097152 | bytes 2622470 | tf_op jit(solution)/shard_map/scatter | solution.py:85
  39.9 40.9 %all_to_all.20 = bf16[64,32,256]{2,1,0:T(8,128)(2,1)S(1)} all-to-all(bf16[64,32,256]{2,1,0:T(8,128)(2,1)S(1)} %bitcast.64), channel_id=1, replica_groups=mesh['dp'=4,'expert'=64] {'expert'}, dimensions={0} | all-to-all | bytes 2097152 | tf_op jit(solution)/shard_map/all_to_all | solution.py:90
  80.9 9.8 %multiply_convert_fusion.1 = (bf16[2048,2048]{1,0:T(8,128)(2,1)S(1)}, f32[2048,2048]{1,0:T(8,128)}) fusion(bf16[2048,256]{1,0:T(8,128)(2,1)S(1)} %bitcast.59, bf16[1,2,256,2048]{3,2,1,0:T(8,128)(2,1)} %all-gather.2.cloned.1.call-done), kind=kOutput, calls=%fused_computation.6 | convolution fusion | flops 2168455168 | bytes 27262976 | tf_op jit(solution)/shard_map/dot_general | solution.py:20
  90.7 3.2 copy-done.2
  93.9 3.8 fusion.1
  97.7 6.5 %all-to-all-start.1 = ((f32[64,32,256]{2,1,0:T(8,128)}), f32[64,32,256]{2,1,0:T(8,128)S(1)}, u32[]{:S(2)}, u32[]{:S(2)}) async-start(f32[64,32,256]{2,1,0:T(8,128)} %fusion.1), calls=%async_computation.1 | async-start | bytes 4194304 | tf_op jit(solution)/shard_map/all_to_all | solution.py:94
  104.2 0.2 reduce-scatter.2.cloned.1.call-start
  104.4 49.4 %all-to-all-done.1 = f32[64,32,256]{2,1,0:T(8,128)S(1)} async-done(((f32[64,32,256]{2,1,0:T(8,128)}), f32[64,32,256]{2,1,0:T(8,128)S(1)}, u32[]{:S(2)}, u32[]{:S(2)}) %all-to-all-start.1) | async-done | bytes 2097184 | tf_op jit(solution)/shard_map/all_to_all | solution.py:94
  153.8 3.5 gather_fusion.1
  157.3 5.7 %scatter_custom_fusion.1 = bf16[2048,256]{1,0:T(8,128)(2,1)S(1)} fusion(s32[1024]{0:T(1024)S(1)} %bitcast.72, f32[1024,256]{1,0:T(8,128)S(1)} %gather_fusion.1, bf16[1024,256]{1,0:T(8,128)(2,1)} %param.11, f32[]{:T(128)} %constant.16.clone.1, bf16[]{:T(256)} %constant.22.clone.1), kind=kCustom, calls=%fused_computation.29 | custom fusion | flops 1048576 | bytes 2621446 | tf_op jit(solution)/shard_map/scatter | solution.py:85
  163.0 34.8 %all_to_all.21 = bf16[64,32,256]{2,1,0:T(8,128)(2,1)S(1)} all-to-all(bf16[64,32,256]{2,1,0:T(8,128)(2,1)S(1)} %bitcast.63), channel_id=1, replica_groups=mesh['dp'=4,'expert'=64] {'expert'}, dimensions={0} | all-to-all | bytes 2097152 | tf_op jit(solution)/shard_map/all_to_all | solution.py:102
  197.8 5.9 %convolution_bitcast_fusion = f32[1,256,2048]{2,1,0:T(8,128)S(1)} fusion(bf16[2048,256]{1,0:T(8,128)(2,1)S(1)} %bitcast.61, bf16[2048,2048]{1,0:T(8,128)(2,1)} %copy-done.2), kind=kOutput, calls=%fused_computation.9 | convolution fusion | flops 2147483648 | bytes 11534336 | tf_op jit(solution)/shard_map/dot_general | solution.py:29
  203.8 10.4 %multiply_convert_fusion = bf16[2048,2048]{1,0:T(8,128)(2,1)S(1)} fusion(f32[2048,2048]{1,0:T(8,128)} %get-tuple-element.9, bf16[2048,256]{1,0:T(8,128)(2,1)S(1)} %bitcast.62, bf16[1,2,256,2048]{3,2,1,0:T(8,128)(2,1)S(1)} %copy-done.14), kind=kOutput, calls=%fused_computation.5 | convolution fusion | flops 2185232384 | bytes 27262976 | tf_op jit(solution)/shard_map/dot_general | solution.py:32
  214.1 3.2 copy-done.3
  217.4 2.3 convolution_bitcast_fusion.1
  219.7 2.2 maximum_bitcast_fusion
  222.0 7.0 %convolution_convert_fusion = bf16[2048,256]{1,0:T(8,128)(2,1)} fusion(bf16[2048,2048]{1,0:T(8,128)(2,1)} %copy-done.3, bf16[1,2,256,2048]{3,2,1,0:T(8,128)(2,1)} %all-gather.2.cloned.1.call-done), kind=kOutput, calls=%fused_computation.11 | convolution fusion | flops 2148007936 | bytes 10485760 | tf_op jit(solution)/shard_map/dot_general | solution.py:37
  229.0 6.6 %all-to-all-start.3 = ((bf16[64,32,256]{2,1,0:T(8,128)(2,1)}), bf16[64,32,256]{2,1,0:T(8,128)(2,1)S(1)}, u32[]{:S(2)}, u32[]{:S(2)}) async-start(bf16[64,32,256]{2,1,0:T(8,128)(2,1)} %bitcast.65), calls=%async_computation.3 | async-start | bytes 2097152 | tf_op jit(solution)/shard_map/all_to_all | solution.py:108
  235.7 0.2 multiply_reduce_fusion
  235.9 0.6 broadcast_multiply_fusion
  236.5 27.1 %all-to-all-done.3 = bf16[64,32,256]{2,1,0:T(8,128)(2,1)S(1)} async-done(((bf16[64,32,256]{2,1,0:T(8,128)(2,1)}), bf16[64,32,256]{2,1,0:T(8,128)(2,1)S(1)}, u32[]{:S(2)}, u32[]{:S(2)}) %all-to-all-start.3) | async-done | bytes 1048608 | tf_op jit(solution)/shard_map/all_to_all | solution.py:108
  263.6 3.9 gather_fusion.2
  267.6 2.7 fusion.12
  270.3 4.3 divide_subtract_fusion
  274.6 249.6 %all-reduce.2.cloned.1.call-done = f32[256,256]{1,0:T(8,128)} async-done(((f32[256,256]{1,0:T(8,128)}), f32[256,256]{1,0:T(8,128)}) %all-reduce.2.cloned.1.call-update) | async-done | bytes 262160 | tf_op jit(solution)/shard_map/psum | solution.py:120
  524.2 1.7 copy.18
  (46 shorter events, 0.8 us)
Async XLA Ops:
  7.2 22.3 %copy-start = (bf16[2048,256]{1,0:T(8,128)(2,1)S(1)}, bf16[2048,256]{1,0:T(8,128)(2,1)}, u32[]{:S(2)}) copy-start(bf16[2048,256]{1,0:T(8,128)(2,1)} %param.8) | copy-start | bytes 3145732
  7.2 26.2 %copy-start.11 = (s32[1024,1]{0,1:T(1,128)S(1)}, s32[1024,1]{0,1:T(1,128)}, u32[]{:S(2)}) copy-start(s32[1024,1]{0,1:T(1,128)} %param.10) | copy-start | bytes 12292
  7.2 26.3 %copy-start.12 = (s32[1024]{0:T(1024)S(1)}, s32[1024]{0:T(1024)}, u32[]{:S(2)}) copy-start(s32[1024]{0:T(1024)} %param.9) | copy-start | bytes 12292
  7.2 26.3 %copy-start.10 = (bf16[256,256]{1,0:T(8,128)(2,1)S(1)}, bf16[256,256]{1,0:T(8,128)(2,1)}, u32[]{:S(2)}) copy-start(bf16[256,256]{1,0:T(8,128)(2,1)} %param.12) | copy-start | bytes 393220
  7.2 73.7 %all-gather.2.cloned.1.call-start = ((), (), s32[]{:S(2)}) async-start(), calls=%async_computation.5 | async-start | bytes 2621440 | tf_op jit(solution)/shard_map/all_gather | solution.py:87
  33.4 57.3 %copy-start.6 = (bf16[1024,256]{1,0:T(8,128)(2,1)}, bf16[1024,256]{1,0:T(8,128)(2,1)S(1)}, u32[]{:S(2)}) copy-start(bf16[1024,256]{1,0:T(8,128)(2,1)S(1)} %gather_fusion) | copy-start | bytes 1572868
  33.9 6.0 %copy-start.8 = (f32[1024,256]{1,0:T(8,128)}, f32[1024,256]{1,0:T(8,128)S(1)}, u32[]{:S(2)}) copy-start(f32[1024,256]{1,0:T(8,128)S(1)} %fusion.18) | copy-start | bytes 3145732
  80.9 9.8 %copy-start.4 = (bf16[64,32,256]{2,1,0:T(8,128)(2,1)}, bf16[64,32,256]{2,1,0:T(8,128)(2,1)S(1)}, u32[]{:S(2)}) copy-start(bf16[64,32,256]{2,1,0:T(8,128)(2,1)S(1)} %all_to_all.20) | copy-start | bytes 3145732
  80.9 13.0 %copy-start.13 = (bf16[1,2,256,2048]{3,2,1,0:T(8,128)(2,1)S(1)}, bf16[1,2,256,2048]{3,2,1,0:T(8,128)(2,1)}, u32[]{:S(2)}) copy-start(bf16[1,2,256,2048]{3,2,1,0:T(8,128)(2,1)} %all-gather.2.cloned.1.call-done) | copy-start | bytes 6291460
  90.7 3.2 copy-start.2
  97.7 56.1 %all-to-all-start.1 = ((f32[64,32,256]{2,1,0:T(8,128)}), f32[64,32,256]{2,1,0:T(8,128)S(1)}, u32[]{:S(2)}, u32[]{:S(2)}) async-start(f32[64,32,256]{2,1,0:T(8,128)} %fusion.1), calls=%async_computation.1 | async-start | bytes 4194304 | tf_op jit(solution)/shard_map/all_to_all | solution.py:94
  104.2 166.2 %reduce-scatter.2.cloned.1.call-start = ((), (), s32[]{:S(2)}) async-start(), calls=%async_computation.7 | async-start | bytes 5242880 | tf_op jit(solution)/shard_map/reduce_scatter | solution.py:122
  197.8 5.9 %copy-start.14 = (bf16[1,2,256,2048]{3,2,1,0:T(8,128)(2,1)S(1)}, bf16[1,2,256,2048]{3,2,1,0:T(8,128)(2,1)}, u32[]{:S(2)}) copy-start(bf16[1,2,256,2048]{3,2,1,0:T(8,128)(2,1)} %all-gather.2.cloned.1.call-done) | copy-start | bytes 6291460
  203.7 13.6 %copy-start.5 = (bf16[64,32,256]{2,1,0:T(8,128)(2,1)S(1)}, bf16[64,32,256]{2,1,0:T(8,128)(2,1)}, u32[]{:S(2)}) copy-start(bf16[64,32,256]{2,1,0:T(8,128)(2,1)} %copy-done.4) | copy-start | bytes 3145732
  214.1 3.2 copy-start.3
  222.0 13.7 %copy-start.9 = (bf16[1024,256]{1,0:T(8,128)(2,1)S(1)}, bf16[1024,256]{1,0:T(8,128)(2,1)}, u32[]{:S(2)}) copy-start(bf16[1024,256]{1,0:T(8,128)(2,1)} %param.11) | copy-start | bytes 1572868
  229.0 38.5 %copy-start.7 = (bf16[1024,256]{1,0:T(8,128)(2,1)S(1)}, bf16[1024,256]{1,0:T(8,128)(2,1)}, u32[]{:S(2)}) copy-start(bf16[1024,256]{1,0:T(8,128)(2,1)} %copy-done.6) | copy-start | bytes 1572868
  229.0 34.6 %all-to-all-start.3 = ((bf16[64,32,256]{2,1,0:T(8,128)(2,1)}), bf16[64,32,256]{2,1,0:T(8,128)(2,1)S(1)}, u32[]{:S(2)}, u32[]{:S(2)}) async-start(bf16[64,32,256]{2,1,0:T(8,128)(2,1)} %bitcast.65), calls=%async_computation.3 | async-start | bytes 2097152 | tf_op jit(solution)/shard_map/all_to_all | solution.py:108
  235.6 288.6 %all-reduce.2.cloned.1.call-start = ((), (), s32[]{:S(2)}) async-start(), calls=%async_computation.6 | async-start | bytes 524288 | tf_op jit(solution)/shard_map/psum | solution.py:120
  263.6 262.3 %copy-start.1 = (bf16[2048,256]{1,0:T(8,128)(2,1)S(1)}, bf16[2048,256]{1,0:T(8,128)(2,1)}, u32[]{:S(2)}) copy-start(bf16[2048,256]{1,0:T(8,128)(2,1)} %param.8) | copy-start | bytes 3145732
Sparse Core Ops, SparseCore 0:
  10.4 37.1 all-gather.1
  222.1 46.4 reduce-scatter.1
  275.6 248.5 all-reduce.1
where the time goes:
time: 533 us; the launch traced here: 532 us
  waiting for transfers between devices  326 us (61%)
  blocking collectives  75.7 us (14%)
  matrix products  42.3 us (8%)
  other arithmetic  40.9 us (8%)
  local copies, waits for them, and re-layouts  19.9 us (4%)
  between operations  14 us (3%)
  starting transfers between devices  13.4 us (3%)
    psum x1, waiting for transfers between devices, on_device(): trunk_grad = lax.psum(trunk_local, ('dp', 'expert'))  250 us
    all_to_all x1, waiting for transfers between devices, on_device(): lax.all_to_all(predicted.reshape(experts, capacity, width), 'expert', spl...  49.4 us
    all_to_all x1, blocking collectives, on_device(): lax.all_to_all(pack(trunk_out), 'expert', split_axis=0, concat_axis=0, ti...  40.9 us
    all_to_all x1, blocking collectives, on_device(): lax.all_to_all(pack(row_error), 'expert', split_axis=0, concat_axis=0, ti...  34.8 us
    all_to_all x1, waiting for transfers between devices, on_device(): lax.all_to_all(input_grad.reshape(experts, capacity, width), 'expert', sp...  27.1 us
    another operation x3, other arithmetic  18.2 us
    scatter x2, other arithmetic, pack(): empty.at[places].set(values).reshape((experts, capacity) + values.shape[1:])  11.7 us
  transfers between devices with their start and end apart: 5, of which 3 were waited for; matrix products, arithmetic and copies ran while one was open for 9% of the time, Pallas kernels for 0%

commit v1 on v0

v1 whole, which is shorter than its diff:
```python
import jax
import jax.numpy as jnp
from jax import lax
from jax.sharding import PartitionSpec as P

loss_scale = 1.0 / 32.0
beta_one = 0.9
beta_two = 0.999
learn_rate = 0.05
adam_eps = 1e-08
adam_step = 10


def silu_slope(values):
    sigma = jax.nn.sigmoid(values)
    return sigma * (1.0 + values * (1.0 - sigma))


def adam_update(params, first, second, grads):
    first_new = beta_one * first + (1.0 - beta_one) * grads
    second_new = beta_two * second + (1.0 - beta_two) * grads * grads
    first_hat = first_new / (1.0 - beta_one**adam_step)
    second_hat = second_new / (1.0 - beta_two**adam_step)
    return (
        params - learn_rate * first_hat / (jnp.sqrt(second_hat) + adam_eps),
        first_new,
        second_new,
    )


def on_device(
    cell_table,
    sample_index,
    region,
    targets,
    trunk_weight,
    expert_params,
    first_moment,
    second_moment,
):
    rows = sample_index.shape[0]
    width = cell_table.shape[1]
    experts = lax.axis_size("expert")
    capacity = 2 * rows // experts
    features = jnp.take(cell_table, sample_index, axis=0)
    routed = region[:, 0]
    onehot = (routed[:, None] == jnp.arange(experts, dtype=jnp.int32)[None, :]).astype(jnp.int32)
    slots = jnp.sum(jnp.cumsum(onehot, axis=0) * onehot, axis=1) - 1
    places = routed * capacity + slots

    gathered = lax.all_gather(expert_params.astype(jnp.bfloat16), "dp", axis=3, tiled=True)
    w_up = gathered[0, 0]
    w_down = gathered[0, 1]

    payload = jnp.concatenate([features, targets], axis=1)
    packed = jnp.zeros((experts * capacity, 2 * width), jnp.bfloat16).at[places].set(payload)
    arrived = lax.all_to_all(
        packed.reshape(experts, capacity, 2 * width), "expert", split_axis=0, concat_axis=0, tiled=True
    ).reshape(-1, 2 * width)
    feats = arrived[:, :width]
    there = arrived[:, width:]

    trunk_pre = jnp.dot(feats, trunk_weight, preferred_element_type=jnp.float32)
    trunk_out = (feats.astype(jnp.float32) + jax.nn.silu(trunk_pre)).astype(jnp.bfloat16)
    up_pre = jnp.dot(trunk_out, w_up, preferred_element_type=jnp.float32)
    hidden = jax.nn.silu(up_pre).astype(jnp.bfloat16)
    predicted = lax.dot_general(
        hidden, w_down, (((1,), (1,)), ((), ())), preferred_element_type=jnp.float32
    )
    errors = predicted - there.astype(jnp.float32)
    losses = jnp.sum(errors * errors, axis=1) * (0.5 * loss_scale)
    scaled = (errors * loss_scale).astype(jnp.bfloat16)
    back = lax.all_to_all(
        losses.reshape(experts, capacity), "expert", split_axis=0, concat_axis=0, tiled=True
    )
    row_loss = back.reshape(-1)[places]
    grad_down = lax.dot_general(
        scaled, hidden, (((0,), (0,)), ((), ())), preferred_element_type=jnp.float32
    )
    hidden_grad = jnp.dot(scaled, w_down, preferred_element_type=jnp.float32)
    pre_grad = (hidden_grad * silu_slope(up_pre)).astype(jnp.bfloat16)
    grad_up = lax.dot_general(
        trunk_out, pre_grad, (((0,), (0,)), ((), ())), preferred_element_type=jnp.float32
    )
    row_grad = lax.dot_general(
        pre_grad, w_up, (((1,), (1,)), ((), ())), preferred_element_type=jnp.float32
    ).astype(jnp.bfloat16)
    trunk_slope = (row_grad.astype(jnp.float32) * silu_slope(trunk_pre)).astype(jnp.bfloat16)
    trunk_local = lax.dot_general(
        feats, trunk_slope, (((0,), (0,)), ((), ())), preferred_element_type=jnp.float32
    )
    trunk_grad = lax.psum(trunk_local, ("dp", "expert"))
    grads = jnp.stack([grad_up, grad_down])[None]
    grad_shard = lax.psum_scatter(grads, "dp", scatter_dimension=3, tiled=True)
    new_params, new_first, new_second = adam_update(
        expert_params, first_moment, second_moment, grad_shard
    )
    return (trunk_grad, row_loss, new_params, new_first, new_second)


def solution(mesh):
    placed = (
        P(("dp", "expert"), None),
        P(("dp", "expert")),
        P(("dp", "expert"), None),
        P(("dp", "expert"), None),
        P(),
        P("expert", None, None, "dp"),
        P("expert", None, None, "dp"),
        P("expert", None, None, "dp"),
    )
    return jax.shard_map(
        on_device,
        mesh=mesh,
        in_specs=placed,
        out_specs=(
            P(),
            P(("dp", "expert")),
            P("expert", None, None, "dp"),
            P("expert", None, None, "dp"),
            P("expert", None, None, "dp"),
        ),
        check_vma=False,
    )
```

time: 533 us -> 452 us (0.85)
  blocking collectives: 75.7 us -> 0 us
  waiting for transfers between devices: 326 us -> 318 us
  starting transfers between devices: 13.4 us -> 20.7 us
    all_to_all x2 -> x0, blocking collectives: 75.7 us -> none  [the longest x1 40.9 us: on_device(): lax.all_to_all(pack(trunk_out), 'expert', split_axis=0, concat_axis=0, ti...]
    all_to_all x2, waiting for transfers between devices: 76.5 us -> 47.5 us  [the longest x1 47.2 us: on_device(): lax.all_to_all(packed.reshape(experts, capacity, 2 * width), 'expert', sp...]
    reduce_scatter x1, waiting for transfers between devices: 0.02 us -> 18.1 us  [on_device(): grad_shard = lax.psum_scatter(grads, 'dp', scatter_dimension=3, tiled=True)]
    all_to_all x2, starting transfers between devices: 13.1 us -> 20.4 us  [the longest x1 13.2 us: on_device(): lax.all_to_all(packed.reshape(experts, capacity, 2 * width), 'expert', sp...]
    unnamed x31 -> x17, local copies, waits for them, and re-layouts: 8.19 us -> 1.71 us
    scatter x2 -> x1, other arithmetic: 11.7 us -> 6.69 us  [on_device(): jnp.zeros((experts * capacity, 2 * width), jnp.bfloat16).at[places]]
    dot_general x8 -> x7, matrix products: 42.3 us -> 44.9 us  [the longest x1 13.3 us: on_device(): hidden_grad = jnp.dot(scaled, w_down, preferred_element_type=jnp.float32)]
  transfers between devices with their start and end apart: 5 -> 5, of which waited for: 3 -> 4; matrix products, arithmetic and copies ran while one was open for 9% -> 6% of each run, Pallas kernels for 0% -> 0%
where the time goes in v1:
time: 452 us; the launch traced here: 451 us
  waiting for transfers between devices  318 us (70%)
  matrix products  44.9 us (10%)
  other arithmetic  36.1 us (8%)
  starting transfers between devices  20.7 us (5%)
  local copies, waits for them, and re-layouts  17.8 us (4%)
  between operations  13.9 us (3%)
    psum x1, waiting for transfers between devices, on_device(): trunk_grad = lax.psum(trunk_local, ('dp', 'expert'))  252 us
    all_to_all x1, waiting for transfers between devices, on_device(): lax.all_to_all(packed.reshape(experts, capacity, 2 * width), 'expert', sp...  47.2 us
    another operation x3, other arithmetic  18.2 us
    reduce_scatter x1, waiting for transfers between devices, on_device(): grad_shard = lax.psum_scatter(grads, 'dp', scatter_dimension=3, tiled=True)  18.1 us
    dot_general x1, matrix products, on_device(): hidden_grad = jnp.dot(scaled, w_down, preferred_element_type=jnp.float32)  13.3 us
    all_to_all x1, starting transfers between devices, on_device(): lax.all_to_all(packed.reshape(experts, capacity, 2 * width), 'expert', sp...  13.2 us
    gather x1, local copies, waits for them, and re-layouts, on_device(): row_loss = back.reshape(-1)[places]  10.5 us
    dot_general x1, matrix products, on_device(): up_pre = jnp.dot(trunk_out, w_up, preferred_element_type=jnp.float32)  10.2 us
  transfers between devices with their start and end apart: 5, of which 4 were waited for; matrix products, arithmetic and copies ran while one was open for 6% of the time, Pallas kernels for 0%

profile of v1, /device:TPU:1, one launch (start us, length us, event | category | flops | bytes accessed | tf_op | source)
XLA Modules:
  0.0 451.0 jit_solution(14048339895175946293)
XLA Ops:
  7.2 0.8 fusion.17
  8.0 0.7 compare_and_fusion
  8.7 0.7 fusion.16
  9.4 18.0 %reduce-window.6 = s32[64,8,128]{2,1,0:T(8,128)S(1)} reduce-window(s32[64,8,128]{2,1,0:T(8,128)S(1)} %fusion.16, s32[]{:T(128)} %constant.20.clone.1), window={size=1x1x128 pad=0_0x0_0x127_0}, to_apply=%region_0.1 | reduce-window | flops 8323072 | bytes 524292 | tf_op jit(solution)/shard_map/reduce-window
  27.4 0.1 slice.28
  27.5 0.1 copy.17
  27.8 0.1 broadcast_add_fusion
  28.1 3.9 gather_fusion
  32.0 0.2 broadcast_select_fusion
  32.2 6.7 %scatter_custom_fusion = bf16[2048,512]{1,0:T(8,128)(2,1)} fusion(s32[1024]{0:T(1024)S(1)} %bitcast.54, bf16[1024,256]{1,0:T(8,128)(2,1)S(1)} %copy-done.4, bf16[]{:T(256)} %constant.67, bf16[1024,256]{1,0:T(8,128)(2,1)S(1)} %broadcast_select_fusion, bf16[]{:T(256)} %constant.18.clone.1), kind=kCustom, calls=%fused_computation.22 | custom fusion | flops 2097152 | bytes 3145732 | tf_op jit(solution)/shard_map/scatter | solution.py:56
  38.9 13.2 %all-to-all-start = ((bf16[64,32,512]{2,1,0:T(8,128)(2,1)}), bf16[64,32,512]{2,1,0:T(8,128)(2,1)S(1)}, u32[]{:S(2)}, u32[]{:S(2)}) async-start(bf16[64,32,512]{2,1,0:T(8,128)(2,1)} %bitcast.6), calls=%async_computation | async-start | bytes 4194304 | tf_op jit(solution)/shard_map/all_to_all | solution.py:57
  52.2 2.1 convert_element_type.38
  54.3 0.2 reduce-scatter.2.cloned.1.call-start
  54.5 47.2 %all-to-all-done = bf16[64,32,512]{2,1,0:T(8,128)(2,1)S(1)} async-done(((bf16[64,32,512]{2,1,0:T(8,128)(2,1)}), bf16[64,32,512]{2,1,0:T(8,128)(2,1)S(1)}, u32[]{:S(2)}, u32[]{:S(2)}) %all-to-all-start) | async-done | bytes 2097184 | tf_op jit(solution)/shard_map/all_to_all | solution.py:57
  101.8 1.7 fusion.12
  103.5 10.2 %multiply_convert_fusion.1 = (bf16[2048,2048]{1,0:T(8,128)(2,1)S(1)}, f32[2048,2048]{1,0:T(8,128)}) fusion(bf16[1,2,256,2048]{3,2,1,0:T(8,128)(2,1)} %all-gather.2.cloned.1.call-done, f32[2048,256]{1,0:T(8,128)} %fusion.12, bf16[2048,512]{1,0:T(8,128)(2,1)S(1)} %bitcast.46), kind=kOutput, calls=%fused_computation.4 | convolution fusion | flops 2172125184 | bytes 29360128 | tf_op jit(solution)/shard_map/dot_general | solution.py:65
  113.7 2.6 multiply_reduce_fusion
  116.3 2.3 convolution_bitcast_fusion
  118.7 13.3 %multiply_convert_fusion = bf16[2048,2048]{1,0:T(8,128)(2,1)} fusion(f32[2048,2048]{1,0:T(8,128)} %get-tuple-element.9, bf16[1,2,256,2048]{3,2,1,0:T(8,128)(2,1)S(1)} %copy-done.7, f32[2048,256]{1,0:T(8,128)S(1)} %get-tuple-element.11), kind=kOutput, calls=%fused_computation.3 | convolution fusion | flops 2186280960 | bytes 28311552 | tf_op jit(solution)/shard_map/dot_general | solution.py:80
  132.0 5.8 %convolution_bitcast_fusion.1 = f32[1,256,2048]{2,1,0:T(8,128)S(1)} fusion(bf16[2048,2048]{1,0:T(8,128)(2,1)} %multiply_convert_fusion, f32[2048,256]{1,0:T(8,128)S(1)} %copy-done.2, bf16[2048,512]{1,0:T(8,128)(2,1)S(1)} %bitcast.48), kind=kOutput, calls=%fused_computation.8 | convolution fusion | flops 2151153664 | bytes 13631488 | tf_op jit(solution)/shard_map/dot_general | solution.py:82
  137.8 2.2 maximum_bitcast_fusion
  140.0 0.7 mul.111
  140.7 7.2 %all-to-all-start.1 = ((f32[64,1,32]{2,1,0:T(1,128)}), f32[64,1,32]{2,1,0:T(1,128)S(1)}, u32[]{:S(2)}, u32[]{:S(2)}) async-start(f32[64,1,32]{2,1,0:T(1,128)} %bitcast.10), calls=%async_computation.1 | async-start | bytes 65536 | tf_op jit(solution)/shard_map/all_to_all | solution.py:73
  148.0 9.0 %fusion.9 = f32[256,256]{1,0:T(8,128)} fusion(bf16[2048,2048]{1,0:T(8,128)(2,1)} %multiply_convert_fusion, f32[2048,256]{1,0:T(8,128)} %fusion.12, bf16[1,2,256,2048]{3,2,1,0:T(8,128)(2,1)} %all-gather.2.cloned.1.call-done, bf16[2048,512]{1,0:T(8,128)(2,1)S(1)} %bitcast.49), kind=kOutput, calls=%fused_computation.29 | convolution fusion | flops 2421686272 | bytes 12845056 | tf_op jit(solution)/shard_map/dot_general | solution.py:89
  157.0 0.3 all-to-all-done.1
  157.3 0.5 broadcast.88
  157.8 0.7 reduce.3
  158.6 10.5 %gather_fusion.1 = f32[1024]{0:T(1024)} fusion(f32[2048]{0:T(1024)S(1)} %reshape.69, s32[1024]{0:T(1024)S(1)} %broadcast_clamp_fusion), kind=kCustom, calls=%fused_computation.1 | custom fusion | bytes 12288 | tf_op jit(solution)/shard_map/gather | solution.py:76
  169.1 18.1 %reduce-scatter.2.cloned.1.call-done = f32[1,2,256,512]{3,2,1,0:T(8,128)} async-done(((f32[1,2,256,2048]{3,2,1,0:T(8,128)}), f32[1,2,256,512]{3,2,1,0:T(8,128)}) %reduce-scatter.2.cloned.1.call-update) | async-done | bytes 1048592 | tf_op jit(solution)/shard_map/reduce_scatter | solution.py:94
  187.2 3.7 divide_subtract_fusion
  190.9 251.9 %all-reduce.2.cloned.1.call-done = f32[256,256]{1,0:T(8,128)} async-done(((f32[256,256]{1,0:T(8,128)}), f32[256,256]{1,0:T(8,128)}) %all-reduce.2.cloned.1.call-update) | async-done | bytes 262160 | tf_op jit(solution)/shard_map/psum | solution.py:92
  442.8 1.7 copy.25
  (31 shorter events, 0.5 us)
Async XLA Ops:
  7.2 20.9 %copy-start = (bf16[2048,256]{1,0:T(8,128)(2,1)S(1)}, bf16[2048,256]{1,0:T(8,128)(2,1)}, u32[]{:S(2)}) copy-start(bf16[2048,256]{1,0:T(8,128)(2,1)} %param.8) | copy-start | bytes 3145732
  7.2 20.8 %copy-start.6 = (s32[1024,1]{0,1:T(1,128)S(1)}, s32[1024,1]{0,1:T(1,128)}, u32[]{:S(2)}) copy-start(s32[1024,1]{0,1:T(1,128)} %param.10) | copy-start | bytes 12292
  28.1 4.2 copy-start.4
  38.9 62.8 %all-to-all-start = ((bf16[64,32,512]{2,1,0:T(8,128)(2,1)}), bf16[64,32,512]{2,1,0:T(8,128)(2,1)S(1)}, u32[]{:S(2)}, u32[]{:S(2)}) async-start(bf16[64,32,512]{2,1,0:T(8,128)(2,1)} %bitcast.6), calls=%async_computation | async-start | bytes 4194304 | tf_op jit(solution)/shard_map/all_to_all | solution.py:57
  52.1 49.7 %copy-start.5 = (bf16[256,256]{1,0:T(8,128)(2,1)S(1)}, bf16[256,256]{1,0:T(8,128)(2,1)}, u32[]{:S(2)}) copy-start(bf16[256,256]{1,0:T(8,128)(2,1)} %param.12) | copy-start | bytes 393220
  52.1 51.4 %all-gather.2.cloned.1.call-start = ((), (), s32[]{:S(2)}) async-start(), calls=%async_computation.3 | async-start | bytes 2621440 | tf_op jit(solution)/shard_map/all_gather | solution.py:51
  54.3 132.9 %reduce-scatter.2.cloned.1.call-start = ((), (), s32[]{:S(2)}) async-start(), calls=%async_computation.5 | async-start | bytes 5242880 | tf_op jit(solution)/shard_map/reduce_scatter | solution.py:94
  103.5 10.2 %copy-start.7 = (bf16[1,2,256,2048]{3,2,1,0:T(8,128)(2,1)S(1)}, bf16[1,2,256,2048]{3,2,1,0:T(8,128)(2,1)}, u32[]{:S(2)}) copy-start(bf16[1,2,256,2048]{3,2,1,0:T(8,128)(2,1)} %all-gather.2.cloned.1.call-done) | copy-start | bytes 6291460
  118.6 13.3 %copy-start.2 = (f32[2048,256]{1,0:T(8,128)S(1)}, f32[2048,256]{1,0:T(8,128)}, u32[]{:S(2)}) copy-start(f32[2048,256]{1,0:T(8,128)} %fusion.12) | copy-start | bytes 6291460
  140.7 16.5 %all-to-all-start.1 = ((f32[64,1,32]{2,1,0:T(1,128)}), f32[64,1,32]{2,1,0:T(1,128)S(1)}, u32[]{:S(2)}, u32[]{:S(2)}) async-start(f32[64,1,32]{2,1,0:T(1,128)} %bitcast.10), calls=%async_computation.1 | async-start | bytes 65536 | tf_op jit(solution)/shard_map/all_to_all | solution.py:73
  148.0 294.8 %all-reduce.2.cloned.1.call-start = ((), (), s32[]{:S(2)}) async-start(), calls=%async_computation.4 | async-start | bytes 524288 | tf_op jit(solution)/shard_map/psum | solution.py:92
  158.6 28.6 %copy-start.1 = (f32[1,2,256,512]{3,2,1,0:T(8,128)S(1)}, f32[1,2,256,512]{3,2,1,0:T(8,128)}, u32[]{:S(2)}) copy-start(f32[1,2,256,512]{3,2,1,0:T(8,128)} %param.13) | copy-start | bytes 3145732
  158.6 28.6 %copy-start.3 = (f32[1,2,256,512]{3,2,1,0:T(8,128)S(1)}, f32[1,2,256,512]{3,2,1,0:T(8,128)}, u32[]{:S(2)}) copy-start(f32[1,2,256,512]{3,2,1,0:T(8,128)} %param.14) | copy-start | bytes 3145732
Sparse Core Ops, SparseCore 0:
  55.3 34.2 all-gather.1
  140.1 47.0 reduce-scatter.1
  194.1 248.5 all-reduce.1

commit v2 on v1

v2 whole, which is shorter than its diff:
```python
import jax
import jax.numpy as jnp
from jax import lax
from jax.experimental import pallas as pl
from jax.experimental.pallas import tpu as pltpu
from jax.sharding import PartitionSpec as P

MESH = pl.DeviceIdType.MESH
bf16 = jnp.bfloat16
f32 = jnp.float32
i32 = jnp.int32

loss_scale = 1.0 / 32.0
beta_one = 0.9
beta_two = 0.999
learn_rate = 0.05
adam_eps = 1e-08
adam_step = 10

NZ, NY, NC, NX = 8, 4, 2, 4
PLANE = NZ * NY * NC
GROUP = NY * NC
D = 256
ROWS = 1024
CELLS = 2048
CAP = 32
CHUNK = GROUP * CAP
SHARE = 512


def adam_update(params, first, second, grads):
    first_new = beta_one * first + (1.0 - beta_one) * grads
    second_new = beta_two * second + (1.0 - beta_two) * grads * grads
    first_hat = first_new / (1.0 - beta_one**adam_step)
    second_hat = second_new / (1.0 - beta_two**adam_step)
    return (
        params - learn_rate * first_hat / (jnp.sqrt(second_hat) + adam_eps),
        first_new,
        second_new,
    )


def dot(a, b):
    return jnp.dot(a, b, preferred_element_type=f32)


def sigmoid(v):
    return 0.5 + 0.5 * jnp.tanh(0.5 * v)


def onehot(mask):
    return jnp.where(mask, 1.0, 0.0).astype(bf16)


def order_of(t):
    return (4 + (1 - 2 * (t % 2)) * ((t + 1) // 2)) % NZ


def fused(
    table, sidx, region, targets, wt, params,
    gout, loss_out, tg_out,
    send, recv, w, wt_t, g, pay, qrow, place, hbuf, sbuf, tacc,
    rs_s, rs_r, ptile, prx, xr, agb, lsend, lrecv,
    a2a_ss, a2a_rs, ag_ss, ag_rs, l_ss, l_rs, r_ss, r_rs, p_ss, p_rs, x_ss, x_rs, b_ss, b_rs,
):
    me = lax.axis_index("expert")
    mx = lax.axis_index("dp")
    mz = me // GROUP
    my = (me // NC) % NY
    mc = me % NC

    def peer(o):
        return ((mz + o // GROUP) % NZ) * GROUP + ((my + (o // NC) % NY) % NY) * NC + (mc + o % NC) % NC

    def source(o):
        return (
            ((mz + NZ - o // GROUP) % NZ) * GROUP
            + ((my + NY - (o // NC) % NY) % NY) * NC
            + (mc + NC - o % NC) % NC
        )

    def plane_copy(src, dst, ss, rs, to):
        return pltpu.make_async_remote_copy(
            src_ref=src, dst_ref=dst, send_sem=ss, recv_sem=rs,
            device_id={"expert": to}, device_id_type=MESH,
        )

    def dp_copy(src, dst, ss, rs, shift):
        return pltpu.make_async_remote_copy(
            src_ref=src, dst_ref=dst, send_sem=ss, recv_sem=rs,
            device_id={"dp": (mx + shift) % NX}, device_id_type=MESH,
        )

    barrier = pltpu.get_barrier_semaphore()

    @pl.loop(1, PLANE)
    def _(o):
        pl.semaphore_signal(barrier, inc=1, device_id={"expert": peer(o)}, device_id_type=MESH)

    for shift in (1, 2, 3):
        pl.semaphore_signal(
            barrier, inc=1, device_id={"dp": (mx + shift) % NX}, device_id_type=MESH
        )

    w[0] = params[...].astype(bf16)
    pl.semaphore_wait(barrier, PLANE - 1 + NX - 1)

    gather = [
        dp_copy(w.at[0, 0], w.at[3, 0], ag_ss.at[0], ag_rs.at[0], 1),
        dp_copy(w.at[0, 1], w.at[1, 1], ag_ss.at[1], ag_rs.at[1], 3),
        dp_copy(w.at[0, 1], w.at[3, 1], ag_ss.at[2], ag_rs.at[2], 1),
        dp_copy(w.at[0, 0], w.at[1, 0], ag_ss.at[3], ag_rs.at[3], 3),
        dp_copy(w.at[3, 0], w.at[2, 0], ag_ss.at[4], ag_rs.at[4], 1),
        dp_copy(w.at[1, 1], w.at[2, 1], ag_ss.at[5], ag_rs.at[5], 3),
    ]
    for copy in gather[:4]:
        copy.start()

    named = region[...]
    q = (
        (((named >> 3) - mz) & (NZ - 1)) * GROUP
        + ((((named >> 1) & (NY - 1)) - my) & (NY - 1)) * NC
        + (((named & 1) - mc) & (NC - 1))
    )
    qrow[...] = q
    before = onehot(
        lax.broadcasted_iota(i32, (256, 256), 0) < lax.broadcasted_iota(i32, (256, 256), 1)
    )
    carry = jnp.zeros((PLANE, 1), f32)
    for b in range(ROWS // 256):
        part = q[:, 256 * b : 256 * b + 256]
        hot = jnp.where(lax.broadcasted_iota(i32, (PLANE, 256), 0) == part, 1.0, 0.0)
        count = dot(hot.astype(bf16), before) + carry
        slot = jnp.sum(hot * count, axis=0, keepdims=True)
        carry = carry + jnp.sum(hot, axis=1, keepdims=True)
        place[:, 256 * b : 256 * b + 256] = part * CAP + slot.astype(i32)

    for b in range(ROWS // 256):
        cols = [
            jnp.transpose(
                jnp.broadcast_to(
                    sidx[:, 256 * b + 128 * h : 256 * b + 128 * h + 128].astype(f32), (128, 128)
                )
            )
            for h in range(2)
        ]
        col = jnp.concatenate(cols, axis=0).astype(i32)
        wide = jnp.concatenate([col] * (CELLS // 128), axis=1)
        pick = onehot(wide == lax.broadcasted_iota(i32, (256, CELLS), 1))
        pay[256 * b : 256 * b + 256, :D] = dot(pick, table[...]).astype(bf16)
    pay[:, D:] = targets[...]

    @pl.loop(0, NZ)
    def _(t):
        dz = order_of(t)
        base = pl.multiple_of(dz * CHUNK, CHUNK)
        mask = lax.broadcasted_iota(i32, (CHUNK, ROWS), 0) + base == place[...]
        send[pl.ds(base, CHUNK), :] = dot(onehot(mask), pay[...]).astype(bf16)

        @pl.loop(0, GROUP)
        def _(i):
            o = dz * GROUP + i

            @pl.when(o != 0)
            def _():
                rows = pl.ds(pl.multiple_of(o * CAP, CAP), CAP)
                plane_copy(
                    send.at[rows], recv.at[rows], a2a_ss.at[dz], a2a_rs.at[dz], peer(o)
                ).start()

    recv[0:CAP, :] = send[0:CAP, :]
    g[...] = jnp.zeros_like(g)
    tacc[...] = jnp.zeros_like(tacc)

    def flip(k, m):
        wt_t[k, m] = jnp.transpose(w[k, m])

    gather[0].wait_recv()
    gather[4].start()
    gather[1].wait_recv()
    gather[5].start()
    flip(0, 0)
    flip(0, 1)
    flip(3, 0)
    flip(1, 1)
    gather[2].wait_recv()
    flip(3, 1)
    gather[3].wait_recv()
    flip(1, 0)
    gather[4].wait_recv()
    flip(2, 0)
    gather[5].wait_recv()
    flip(2, 1)

    reduce = [
        dp_copy(rs_s.at[n], rs_r.at[n], r_ss.at[n], r_rs.at[n], 1 if n in (0, 2, 4) else 3)
        for n in range(6)
    ]

    def chunk_wait(dz):
        @pl.when(dz != 0)
        def _():
            rows = pl.ds(pl.multiple_of(dz * CHUNK, CHUNK), CHUNK)
            plane_copy(send.at[rows], recv.at[rows], a2a_ss.at[dz], a2a_rs.at[dz], me).wait_recv()

        @pl.when(dz == 0)
        def _():
            rows = pl.ds(CAP, CHUNK - CAP)
            plane_copy(send.at[rows], recv.at[rows], a2a_ss.at[0], a2a_rs.at[0], me).wait_recv()

    @pl.loop(0, NZ)
    def _(t):
        dz = order_of(t)
        chunk_wait(dz)
        rows = pl.ds(pl.multiple_of(dz * CHUNK, CHUNK), CHUNK)
        feats = recv[rows, :D]
        feats_f = feats.astype(f32)
        trunk_pre = dot(feats, wt[...])
        trunk_sig = sigmoid(trunk_pre)
        trunk_f = feats_f + trunk_pre * trunk_sig
        trunk_out = trunk_f.astype(bf16)
        trunk_t = jnp.transpose(trunk_f).astype(bf16)
        predicted = jnp.zeros((CHUNK, D), f32)
        for k in range(NX):
            up = dot(trunk_out, w[k, 0])
            sig = sigmoid(up)
            hid = up * sig
            hid_b = hid.astype(bf16)
            hbuf[k] = hid_b
            sbuf[k] = sig + hid * (1.0 - sig)
            predicted = predicted + dot(hid_b, wt_t[k, 1])
        errors = predicted - recv[rows, D:].astype(f32)
        squares = errors * errors
        squares = jnp.transpose(squares[:, :128] + squares[:, 128:])
        lsend[dz] = jnp.sum(squares, axis=0, keepdims=True) * (0.5 * loss_scale)

        @pl.loop(0, GROUP)
        def _(i):
            o = dz * GROUP + i

            @pl.when(o != 0)
            def _():
                plane_copy(lsend.at[dz], lrecv.at[o], l_ss, l_rs, source(o)).start()

        scaled_f = errors * loss_scale
        scaled = scaled_f.astype(bf16)
        scaled_t = jnp.transpose(scaled_f).astype(bf16)
        row_grad = jnp.zeros((CHUNK, D), f32)
        for k in (2, 1, 3, 0):
            pre_grad = (dot(scaled, w[k, 1]) * sbuf[k]).astype(bf16)
            g[k, 0] += dot(trunk_t, pre_grad)
            g[k, 1] += dot(scaled_t, hbuf[k])
            if k:

                @pl.when(t == NZ - 1)
                def _():
                    for n, m in {2: ((0, 0), (1, 1)), 1: ((2, 1),), 3: ((3, 0),)}[k]:
                        rs_s[n] = g[k, m].astype(bf16)
                        reduce[n].start()

            row_grad = row_grad + dot(pre_grad, wt_t[k, 0])
        slope = trunk_sig + trunk_pre * trunk_sig * (1.0 - trunk_sig)
        trunk_slope = (row_grad.astype(bf16).astype(f32) * slope).astype(bf16)
        tacc[...] += dot(jnp.transpose(feats_f).astype(bf16), trunk_slope)

    for p in range(PLANE):
        ptile[p] = tacc[8 * (p % 32) : 8 * (p % 32) + 8, 128 * (p // 32) : 128 * (p // 32) + 128]

    @pl.loop(1, PLANE)
    def _(o):
        to = peer(o)
        plane_copy(ptile.at[to], prx.at[o], p_ss, p_rs, to).start()

    prx[0] = ptile[me]
    lrecv[0] = lsend[0]

    reduce[0].wait_recv()
    rs_s[4] = (g[1, 0] + rs_r[0].astype(f32)).astype(bf16)
    reduce[4].start()
    reduce[1].wait_recv()
    rs_s[5] = (g[3, 1] + rs_r[1].astype(f32)).astype(bf16)
    reduce[5].start()

    others = pl.ds(1, PLANE - 1)
    plane_copy(ptile.at[others], prx.at[others], p_ss, p_rs, me).wait_recv()
    xr[mx] = jnp.sum(prx[...], axis=0)
    for shift in (1, 2, 3):
        dp_copy(xr.at[mx], xr.at[mx], x_ss, x_rs, shift).start()

    plane_copy(lrecv.at[others], lrecv.at[others], l_ss, l_rs, me).wait_recv()
    table_f = lrecv[...].reshape(PLANE, CHUNK)
    high = table_f.astype(bf16)
    rest = table_f - high.astype(f32)
    middle = rest.astype(bf16)
    low = (rest - middle.astype(f32)).astype(bf16)
    spot = place[...] & (CHUNK - 1)
    hot = onehot(lax.broadcasted_iota(i32, (PLANE, ROWS), 0) == qrow[...])
    seen = sum(
        lax.dot_general(part, hot, (((0,), (0,)), ((), ())), preferred_element_type=f32)
        for part in (high, middle, low)
    )
    loss_out[...] = jnp.sum(
        jnp.where(lax.broadcasted_iota(i32, (CHUNK, ROWS), 0) == spot, seen, 0.0),
        axis=0,
        keepdims=True,
    )

    three = pl.ds(0, NX - 1)
    dp_copy(xr.at[three], xr.at[three], x_ss, x_rs, 1).wait_recv()
    agb[me] = (xr[0] + xr[1]) + (xr[2] + xr[3])

    @pl.loop(1, PLANE)
    def _(o):
        plane_copy(agb.at[me], agb.at[me], b_ss, b_rs, peer(o)).start()

    reduce[2].wait_recv()
    reduce[3].wait_recv()
    reduce[4].wait_recv()
    gout[0] = g[0, 0] + rs_r[3].astype(f32) + rs_r[4].astype(f32)
    reduce[5].wait_recv()
    gout[1] = g[0, 1] + rs_r[2].astype(f32) + rs_r[5].astype(f32)

    plane_copy(agb.at[others], agb.at[others], b_ss, b_rs, me).wait_recv()
    for p in range(PLANE):
        tg_out[8 * (p % 32) : 8 * (p % 32) + 8, 128 * (p // 32) : 128 * (p // 32) + 128] = agb[p]

    for dz in range(NZ):
        rows = pl.ds(CAP if dz == 0 else dz * CHUNK, CHUNK - CAP if dz == 0 else CHUNK)
        plane_copy(send.at[rows], recv.at[rows], a2a_ss.at[dz], a2a_rs.at[dz], me).wait_send()
    for copy in gather + reduce:
        copy.wait_send()
    plane_copy(lrecv.at[others], lrecv.at[others], l_ss, l_rs, me).wait_send()
    plane_copy(ptile.at[others], prx.at[others], p_ss, p_rs, me).wait_send()
    plane_copy(agb.at[others], agb.at[others], b_ss, b_rs, me).wait_send()
    dp_copy(xr.at[three], xr.at[three], x_ss, x_rs, 1).wait_send()


def on_device(
    cell_table, sample_index, region, targets, trunk_weight, expert_params, first_moment, second_moment
):
    vmem = pl.BlockSpec(memory_space=pltpu.VMEM)
    dma = pltpu.SemaphoreType.DMA
    grads, losses, trunk_grad = pl.pallas_call(
        fused,
        out_shape=(
            jax.ShapeDtypeStruct((2, D, SHARE), f32),
            jax.ShapeDtypeStruct((1, ROWS), f32),
            jax.ShapeDtypeStruct((D, D), f32),
        ),
        in_specs=[vmem] * 6,
        out_specs=(vmem, vmem, vmem),
        scratch_shapes=[
            pltpu.VMEM((PLANE * CAP, 2 * D), bf16),
            pltpu.VMEM((PLANE * CAP, 2 * D), bf16),
            pltpu.VMEM((NX, 2, D, SHARE), bf16),
            pltpu.VMEM((NX, 2, SHARE, D), bf16),
            pltpu.VMEM((NX, 2, D, SHARE), f32),
            pltpu.VMEM((ROWS, 2 * D), bf16),
            pltpu.VMEM((1, ROWS), i32),
            pltpu.VMEM((1, ROWS), i32),
            pltpu.VMEM((NX, CHUNK, SHARE), bf16),
            pltpu.VMEM((NX, CHUNK, SHARE), f32),
            pltpu.VMEM((D, D), f32),
            pltpu.VMEM((6, D, SHARE), bf16),
            pltpu.VMEM((6, D, SHARE), bf16),
            pltpu.VMEM((PLANE, 8, 128), f32),
            pltpu.VMEM((PLANE, 8, 128), f32),
            pltpu.VMEM((NX, 8, 128), f32),
            pltpu.VMEM((PLANE, 8, 128), f32),
            pltpu.VMEM((NZ, 1, CHUNK), f32),
            pltpu.VMEM((PLANE, 1, CHUNK), f32),
            dma((NZ,)), dma((NZ,)),
            dma((6,)), dma((6,)),
            dma, dma,
            dma((6,)), dma((6,)),
            dma, dma,
            dma, dma,
            dma, dma,
        ],
        compiler_params=pltpu.CompilerParams(
            collective_id=0, has_side_effects=True, vmem_limit_bytes=56 << 20
        ),
        name="fused_step",
    )(
        cell_table,
        sample_index.reshape(1, ROWS),
        region.reshape(1, ROWS),
        targets,
        trunk_weight,
        expert_params[0],
    )
    new_params, new_first, new_second = adam_update(
        expert_params, first_moment, second_moment, grads[None]
    )
    return (trunk_grad, losses.reshape(ROWS), new_params, new_first, new_second)


def solution(mesh):
    placed = (
        P(("dp", "expert"), None),
        P(("dp", "expert")),
        P(("dp", "expert"), None),
        P(("dp", "expert"), None),
        P(),
        P("expert", None, None, "dp"),
        P("expert", None, None, "dp"),
        P("expert", None, None, "dp"),
    )
    return jax.shard_map(
        on_device,
        mesh=mesh,
        in_specs=placed,
        out_specs=(
            P(),
            P(("dp", "expert")),
            P("expert", None, None, "dp"),
            P("expert", None, None, "dp"),
            P("expert", None, None, "dp"),
        ),
        check_vma=False,
    )
```

time: 452 us -> 113 us (0.25)
  waiting for transfers between devices: 318 us -> 0 us
  Pallas kernels: 0 us -> 108 us
  matrix products: 44.9 us -> 0 us
  other arithmetic: 36.1 us -> 3.71 us
  starting transfers between devices: 20.7 us -> 0 us
  local copies, waits for them, and re-layouts: 17.8 us -> 1.31 us
  between operations: 13.9 us -> 0.68 us
    psum x1 -> x0, waiting for transfers between devices: 252 us -> none  [on_device(): trunk_grad = lax.psum(trunk_local, ('dp', 'expert'))]
    pallas_call x0 -> x1, Pallas kernels: none -> 108 us  [on_device(): pl.pallas_call(fused, out_shape=(jax.ShapeDtypeStruct((2, D, SHARE), f32)...]
    all_to_all x2 -> x0, waiting for transfers between devices: 47.5 us -> none  [the longest x1 47.2 us: on_device(): lax.all_to_all(packed.reshape(experts, capacity, 2 * width), 'expert', sp...]
    dot_general x7 -> x0, matrix products: 44.9 us -> none  [the longest x1 13.3 us: on_device(): hidden_grad = jnp.dot(scaled, w_down, preferred_element_type=jnp.float32)]
    all_to_all x2 -> x0, starting transfers between devices: 20.4 us -> none  [the longest x1 13.2 us: on_device(): lax.all_to_all(packed.reshape(experts, capacity, 2 * width), 'expert', sp...]
    another operation x3 -> x0, other arithmetic: 18.2 us -> none
    reduce_scatter x1 -> x0, waiting for transfers between devices: 18.1 us -> none  [on_device(): grad_shard = lax.psum_scatter(grads, 'dp', scatter_dimension=3, tiled=True)]
    gather x2 -> x0, local copies, waits for them, and re-layouts: 14.5 us -> none  [the longest x1 10.5 us: on_device(): row_loss = back.reshape(-1)[places]]
  transfers between devices with their start and end apart: 5 -> 0, of which waited for: 4 -> 0; matrix products, arithmetic and copies ran while one was open for 6% -> 0% of each run, Pallas kernels for 0% -> 0%
where the time goes in v2:
time: 113 us
  Pallas kernels  108 us (96%)
  other arithmetic  3.71 us (3%)
  local copies, waits for them, and re-layouts  1.31 us (1%)
    pallas_call x1, Pallas kernels, on_device(): pl.pallas_call(fused, out_shape=(jax.ShapeDtypeStruct((2, D, SHARE), f32)...  108 us
    sub x1, other arithmetic, adam_update(): params - learn_rate * first_hat / (jnp.sqrt(second_hat) + adam_eps)  3.71 us

profile of v2, /device:TPU:1, one launch (start us, length us, event | category | flops | bytes accessed | tf_op | source)
XLA Modules:
  0.0 113.4 jit_solution(13156911826956609013)
XLA Ops:
  0.6 0.0 copy-start
  0.6 0.0 copy-start.1
  0.7 107.6 %fused_step.1 = (f32[2,256,512]{2,1,0:T(8,128)}, f32[1,1024]{1,0:T(1,128)}, f32[256,256]{1,0:T(8,128)}) custom-call(bf16[2048,256]{1,0:T(8,128)(2,1)} %table.1, s32[1,1024]{1,0:T(1,128)} %bitcast.13, s32[1,1024]{1,0:T(1,128)} %bitcast.14, bf16[1024,256]{1,0:T(8,128)(2,1)} %targets.1, bf16[256,256]{1,0:T(8,128)(2,1)} %wt.1, f32[2,256,512]{2,1,0:T(8,128)} %bitcast.12), custom_call_target="tpu_custom_call" | custom-call | tf_op jit(solution)/shard_map/fused_step/pallas_call | solution.py:343
  108.3 0.0 copy-done
  108.3 0.0 copy-done.1
  108.3 0.0 copy-start.2
  108.3 3.7 %divide_subtract_fusion = (f32[1,2,256,512]{3,2,1,0:T(8,128)}, f32[1,2,256,512]{3,2,1,0:T(8,128)}, f32[1,2,256,512]{3,2,1,0:T(8,128)}) fusion(f32[1,2,256,512]{3,2,1,0:T(8,128)S(1)} %copy-done, f32[2,256,512]{2,1,0:T(8,128)} %get-tuple-element.10, f32[1,2,256,512]{3,2,1,0:T(8,128)S(1)} %copy-done.1, f32[1,2,256,512]{3,2,1,0:T(8,128)} %param.15), kind=kLoop, calls=%fused_computation.4 | loop fusion | flops 3145728 | bytes 7340032 | tf_op jit(solution)/shard_map/sub | solution.py:37
  112.1 0.0 copy-done.2
  112.1 0.0 copy-start.3
  112.1 0.7 copy.15
  112.8 0.0 copy-done.3
  112.8 0.6 copy.16
Async XLA Ops:
  0.6 107.7 %copy-start = (f32[1,2,256,512]{3,2,1,0:T(8,128)S(1)}, f32[1,2,256,512]{3,2,1,0:T(8,128)}, u32[]{:S(2)}) copy-start(f32[1,2,256,512]{3,2,1,0:T(8,128)} %param.13) | copy-start | bytes 3145732
  0.6 107.7 %copy-start.1 = (f32[1,2,256,512]{3,2,1,0:T(8,128)S(1)}, f32[1,2,256,512]{3,2,1,0:T(8,128)}, u32[]{:S(2)}) copy-start(f32[1,2,256,512]{3,2,1,0:T(8,128)} %param.14) | copy-start | bytes 3145732
  108.3 3.7 %copy-start.2 = (f32[256,256]{1,0:T(8,128)S(1)}, f32[256,256]{1,0:T(8,128)}, u32[]{:S(2)}) copy-start(f32[256,256]{1,0:T(8,128)} %get-tuple-element.19) | copy-start | bytes 786436
  112.1 0.7 copy-start.3

commit v3 on v2

v3 whole, which is shorter than its diff:
```python
import jax
import jax.numpy as jnp
from jax import lax
from jax.experimental import pallas as pl
from jax.experimental.pallas import tpu as pltpu
from jax.sharding import PartitionSpec as P

MESH = pl.DeviceIdType.MESH
bf16 = jnp.bfloat16
f32 = jnp.float32
i32 = jnp.int32

loss_scale = 1.0 / 32.0
beta_one = 0.9
beta_two = 0.999
learn_rate = 0.05
adam_eps = 1e-08
adam_step = 10

NZ, NY, NC, NX = 8, 4, 2, 4
PLANE = NZ * NY * NC
GROUP = NY * NC
D = 256
ROWS = 1024
CELLS = 2048
CAP = 32
CHUNK = GROUP * CAP
SHARE = 512


def adam_update(params, first, second, grads):
    first_new = beta_one * first + (1.0 - beta_one) * grads
    second_new = beta_two * second + (1.0 - beta_two) * grads * grads
    first_hat = first_new / (1.0 - beta_one**adam_step)
    second_hat = second_new / (1.0 - beta_two**adam_step)
    return (
        params - learn_rate * first_hat / (jnp.sqrt(second_hat) + adam_eps),
        first_new,
        second_new,
    )


def dot(a, b):
    return jnp.dot(a, b, preferred_element_type=f32)


def sigmoid(v):
    return 0.5 + 0.5 * jnp.tanh(0.5 * v)


def onehot(mask):
    return jnp.where(mask, 1.0, 0.0).astype(bf16)


def fused(
    table, sidx, region, targets, wt, params,
    gout, loss_out, tg_out,
    send, recv, w, wt_t, g, pay, qrow, place, hbuf, sbuf, pbuf, tacc,
    rs_s, rs_r, tr, tz, zr, xr, agz, agb, lsend, lmid, lrecv,
    a_ss, a_rs, ready, ag_ss, ag_rs, r_ss, r_rs, s_ss, s_rs,
):
    me = lax.axis_index("expert")
    mx = lax.axis_index("dp")
    mz = me // GROUP
    my = (me // NC) % NY
    mc = me % NC
    mg = me % GROUP

    def along_z(d):
        return ((mz + d) % NZ) * GROUP + mg

    def in_group(i):
        return mz * GROUP + ((my + i // NC) % NY) * NC + (mc + i % NC) % NC

    def before_in_group(i):
        return mz * GROUP + ((my + NY - i // NC) % NY) * NC + (mc + NC - i % NC) % NC

    def owner(i, d):
        return ((mz + d) % NZ) * GROUP + ((my + i // NC) % NY) * NC + (mc + i % NC) % NC

    def plane_copy(src, dst, ss, rs, to):
        return pltpu.make_async_remote_copy(
            src_ref=src, dst_ref=dst, send_sem=ss, recv_sem=rs,
            device_id={"expert": to}, device_id_type=MESH,
        )

    def dp_copy(src, dst, ss, rs, shift):
        return pltpu.make_async_remote_copy(
            src_ref=src, dst_ref=dst, send_sem=ss, recv_sem=rs,
            device_id={"dp": (mx + shift) % NX}, device_id_type=MESH,
        )

    barrier = pltpu.get_barrier_semaphore()
    for d in (4, 3, 5, 2, 6, 1, 7):
        pl.semaphore_signal(barrier, inc=1, device_id={"expert": along_z(d)}, device_id_type=MESH)
    for i in range(1, GROUP):
        pl.semaphore_signal(barrier, inc=1, device_id={"expert": in_group(i)}, device_id_type=MESH)
    for shift in (1, 2, 3):
        pl.semaphore_signal(
            barrier, inc=1, device_id={"dp": (mx + shift) % NX}, device_id_type=MESH
        )

    w[0] = params[...].astype(bf16)

    named = region[...]
    q = (
        ((((named >> 1) & (NY - 1)) - my) & (NY - 1)) * NC * NZ
        + (((named & 1) - mc) & (NC - 1)) * NZ
        + (((named >> 3) - mz) & (NZ - 1))
    )
    qrow[...] = q
    before = onehot(
        lax.broadcasted_iota(i32, (256, 256), 0) < lax.broadcasted_iota(i32, (256, 256), 1)
    )
    carry = jnp.zeros((PLANE, 1), f32)
    for b in range(ROWS // 256):
        part = q[:, 256 * b : 256 * b + 256]
        hot = jnp.where(lax.broadcasted_iota(i32, (PLANE, 256), 0) == part, 1.0, 0.0)
        count = dot(hot.astype(bf16), before) + carry
        slot = jnp.sum(hot * count, axis=0, keepdims=True)
        carry = carry + jnp.sum(hot, axis=1, keepdims=True)
        place[:, 256 * b : 256 * b + 256] = part * CAP + slot.astype(i32)

    for b in range(ROWS // 256):
        cols = [
            jnp.transpose(
                jnp.broadcast_to(
                    sidx[:, 256 * b + 128 * h : 256 * b + 128 * h + 128].astype(f32), (128, 128)
                )
            )
            for h in range(2)
        ]
        col = jnp.concatenate(cols, axis=0).astype(i32)
        wide = jnp.concatenate([col] * (CELLS // 128), axis=1)
        pick = onehot(wide == lax.broadcasted_iota(i32, (256, CELLS), 1))
        pay[256 * b : 256 * b + 256, :D] = dot(pick, table[...]).astype(bf16)
    pay[:, D:] = targets[...]

    def pack(i):
        mask = lax.broadcasted_iota(i32, (CHUNK, ROWS), 0) + i * CHUNK == place[...]
        send[i] = dot(onehot(mask), pay[...]).astype(bf16)

    def row_copy(i, d):
        rows = pl.ds(d * CAP, CAP)
        return plane_copy(
            send.at[i, rows], recv.at[i, rows], a_ss.at[i], a_rs.at[i], owner(i, d)
        )

    pack(0)
    recv[0, 0:CAP] = send[0, 0:CAP]
    pl.semaphore_wait(barrier, NZ - 1 + GROUP - 1 + NX - 1)
    for d in (4, 3, 5, 2, 6, 1, 7):
        row_copy(0, d).start()

    for i in range(1, GROUP):
        pl.semaphore_signal(ready, inc=1, device_id={"expert": in_group(i)}, device_id_type=MESH)

    gather = [
        dp_copy(w.at[0, 0], w.at[3, 0], ag_ss.at[0], ag_rs.at[0], 1),
        dp_copy(w.at[0, 1], w.at[1, 1], ag_ss.at[1], ag_rs.at[1], 3),
        dp_copy(w.at[0, 1], w.at[3, 1], ag_ss.at[2], ag_rs.at[2], 1),
        dp_copy(w.at[0, 0], w.at[1, 0], ag_ss.at[3], ag_rs.at[3], 3),
        dp_copy(w.at[3, 0], w.at[2, 0], ag_ss.at[4], ag_rs.at[4], 1),
        dp_copy(w.at[1, 1], w.at[2, 1], ag_ss.at[5], ag_rs.at[5], 3),
    ]
    for copy in gather[:4]:
        copy.start()

    pack(1)
    pl.semaphore_wait(ready, GROUP - 1)

    @pl.loop(1, GROUP)
    def _(i):
        for d in (4, 3, 5, 2, 6, 1, 7, 0):
            row_copy(i, d).start()

        @pl.when(i < GROUP - 1)
        def _():
            pack(i + 1)

    g[...] = jnp.zeros_like(g)
    tacc[...] = jnp.zeros_like(tacc)

    def flip(k, m):
        wt_t[k, m] = jnp.transpose(w[k, m])

    gather[0].wait_recv()
    gather[4].start()
    gather[1].wait_recv()
    gather[5].start()
    flip(0, 0)
    flip(0, 1)
    flip(3, 0)
    flip(1, 1)
    gather[2].wait_recv()
    flip(3, 1)
    gather[3].wait_recv()
    flip(1, 0)
    gather[4].wait_recv()
    flip(2, 0)
    gather[5].wait_recv()
    flip(2, 1)

    reduce = [
        dp_copy(rs_s.at[n], rs_r.at[n], r_ss.at[n], r_rs.at[n], 1 if n in (0, 2, 4) else 3)
        for n in range(6)
    ]
    others = pl.ds(1, GROUP - 1)
    rest = pl.ds(CAP, CHUNK - CAP)

    @pl.loop(0, GROUP)
    def _(t):
        @pl.when(t == 0)
        def _():
            plane_copy(send.at[0, rest], recv.at[0, rest], a_ss.at[0], a_rs.at[0], me).wait_recv()

        @pl.when(t != 0)
        def _():
            plane_copy(send.at[t], recv.at[t], a_ss.at[t], a_rs.at[t], me).wait_recv()

        feats = recv[t, :, :D]
        feats_f = feats.astype(f32)
        trunk_pre = dot(feats, wt[...])
        trunk_sig = sigmoid(trunk_pre)
        trunk_f = feats_f + trunk_pre * trunk_sig
        trunk_out = trunk_f.astype(bf16)
        trunk_t = jnp.transpose(trunk_f).astype(bf16)
        predicted = jnp.zeros((CHUNK, D), f32)
        for k in range(NX):
            up = dot(trunk_out, w[k, 0])
            sig = sigmoid(up)
            hid = up * sig
            hid_b = hid.astype(bf16)
            hbuf[k] = hid_b
            sbuf[k] = sig + hid * (1.0 - sig)
            predicted = predicted + dot(hid_b, wt_t[k, 1])
        errors = predicted - recv[t, :, D:].astype(f32)
        squares = errors * errors
        squares = jnp.transpose(squares[:, :128] + squares[:, 128:])
        lsend[t] = jnp.sum(squares, axis=0, keepdims=True) * (0.5 * loss_scale)

        @pl.when(t != 0)
        def _():
            plane_copy(
                lsend.at[t], lmid.at[t], s_ss.at[0], s_rs.at[0], before_in_group(t)
            ).start()

        scaled_f = errors * loss_scale
        scaled = scaled_f.astype(bf16)
        scaled_t = jnp.transpose(scaled_f).astype(bf16)
        row_grad = jnp.zeros((CHUNK, D), f32)
        for k in range(NX):
            pre_grad = (dot(scaled, w[k, 1]) * sbuf[k]).astype(bf16)
            pbuf[k] = pre_grad
            row_grad = row_grad + dot(pre_grad, wt_t[k, 0])
        slope = trunk_sig + trunk_pre * trunk_sig * (1.0 - trunk_sig)
        trunk_slope = (row_grad.astype(bf16).astype(f32) * slope).astype(bf16)
        tacc[...] += dot(jnp.transpose(feats_f).astype(bf16), trunk_slope)

        @pl.when(t == GROUP - 1)
        def _():
            for i in range(1, GROUP):
                to = in_group(i)
                share = pl.ds(pl.multiple_of((to % GROUP) * 32, 32), 32)
                plane_copy(tacc.at[share], tr.at[i], s_ss.at[1], s_rs.at[1], to).start()

        for k in (2, 1, 3, 0):
            g[k, 0] += dot(trunk_t, pbuf[k])
            g[k, 1] += dot(scaled_t, hbuf[k])
            if k:

                @pl.when(t == GROUP - 1)
                def _():
                    for n, m in {2: ((0, 0), (1, 1)), 1: ((2, 1),), 3: ((3, 0),)}[k]:
                        rs_s[n] = g[k, m].astype(bf16)
                        reduce[n].start()

    tr[0] = tacc[pl.ds(pl.multiple_of(mg * 32, 32), 32)]
    lmid[0] = lsend[0]
    plane_copy(tr.at[others], tr.at[others], s_ss.at[1], s_rs.at[1], me).wait_recv()
    total = jnp.sum(tr[...], axis=0)
    for p in range(NZ):
        tz[p] = total[8 * (p % 4) : 8 * (p % 4) + 8, 128 * (p // 4) : 128 * (p // 4) + 128]
    for d in (4, 3, 5, 2, 6, 1, 7):
        plane_copy(tz.at[(mz + d) % NZ], zr.at[d], s_ss.at[2], s_rs.at[2], along_z(d)).start()
    zr[0] = tz[mz]

    plane_copy(lmid.at[others], lmid.at[others], s_ss.at[0], s_rs.at[0], me).wait_recv()
    for d in (4, 3, 5, 2, 6, 1, 7):
        plane_copy(lmid, lrecv.at[d], s_ss.at[3], s_rs.at[3], along_z(NZ - d)).start()
    lrecv[0] = lmid[...]

    reduce[0].wait_recv()
    rs_s[4] = (g[1, 0] + rs_r[0].astype(f32)).astype(bf16)
    reduce[4].start()
    reduce[1].wait_recv()
    rs_s[5] = (g[3, 1] + rs_r[1].astype(f32)).astype(bf16)
    reduce[5].start()

    plane_copy(zr.at[others], zr.at[others], s_ss.at[2], s_rs.at[2], me).wait_recv()
    xr[mx] = jnp.sum(zr[...], axis=0)
    for shift in (1, 2, 3):
        dp_copy(xr.at[mx], xr.at[mx], s_ss.at[4], s_rs.at[4], shift).start()

    three = pl.ds(0, NX - 1)
    dp_copy(xr.at[three], xr.at[three], s_ss.at[4], s_rs.at[4], 1).wait_recv()
    agz[mz] = (xr[0] + xr[1]) + (xr[2] + xr[3])
    for d in (4, 3, 5, 2, 6, 1, 7):
        plane_copy(agz.at[mz], agz.at[mz], s_ss.at[5], s_rs.at[5], along_z(d)).start()

    plane_copy(lrecv.at[others], lrecv.at[others], s_ss.at[3], s_rs.at[3], me).wait_recv()
    table_f = lrecv[...].reshape(PLANE, CHUNK)
    high = table_f.astype(bf16)
    left = table_f - high.astype(f32)
    middle = left.astype(bf16)
    low = (left - middle.astype(f32)).astype(bf16)
    spot = place[...] & (CHUNK - 1)
    turned = (qrow[...] & (NZ - 1)) * GROUP + (qrow[...] >> 3)
    hot = onehot(lax.broadcasted_iota(i32, (PLANE, ROWS), 0) == turned)
    seen = sum(
        lax.dot_general(part, hot, (((0,), (0,)), ((), ())), preferred_element_type=f32)
        for part in (high, middle, low)
    )
    loss_out[...] = jnp.sum(
        jnp.where(lax.broadcasted_iota(i32, (CHUNK, ROWS), 0) == spot, seen, 0.0),
        axis=0,
        keepdims=True,
    )

    plane_copy(agz.at[others], agz.at[others], s_ss.at[5], s_rs.at[5], me).wait_recv()
    for i in range(1, GROUP):
        plane_copy(agz, agb.at[mg], s_ss.at[6], s_rs.at[6], in_group(i)).start()
    agb[mg] = agz[...]

    reduce[2].wait_recv()
    reduce[3].wait_recv()
    reduce[4].wait_recv()
    gout[0] = g[0, 0] + rs_r[3].astype(f32) + rs_r[4].astype(f32)
    reduce[5].wait_recv()
    gout[1] = g[0, 1] + rs_r[2].astype(f32) + rs_r[5].astype(f32)

    plane_copy(agb.at[others], agb.at[others], s_ss.at[6], s_rs.at[6], me).wait_recv()
    for i in range(GROUP):
        for p in range(NZ):
            row, col = 32 * i + 8 * (p % 4), 128 * (p // 4)
            tg_out[row : row + 8, col : col + 128] = agb[i, p]

    plane_copy(send.at[0, rest], recv.at[0, rest], a_ss.at[0], a_rs.at[0], me).wait_send()
    for i in range(1, GROUP):
        plane_copy(send.at[i], recv.at[i], a_ss.at[i], a_rs.at[i], me).wait_send()
    for copy in gather + reduce:
        copy.wait_send()
    for n, ref in ((0, lmid), (1, tr), (2, zr), (3, lrecv), (5, agz), (6, agb)):
        plane_copy(ref.at[others], ref.at[others], s_ss.at[n], s_rs.at[n], me).wait_send()
    dp_copy(xr.at[three], xr.at[three], s_ss.at[4], s_rs.at[4], 1).wait_send()


def on_device(
    cell_table, sample_index, region, targets, trunk_weight, expert_params, first_moment, second_moment
):
    vmem = pl.BlockSpec(memory_space=pltpu.VMEM)
    dma = pltpu.SemaphoreType.DMA
    grads, losses, trunk_grad = pl.pallas_call(
        fused,
        out_shape=(
            jax.ShapeDtypeStruct((2, D, SHARE), f32),
            jax.ShapeDtypeStruct((1, ROWS), f32),
            jax.ShapeDtypeStruct((D, D), f32),
        ),
        in_specs=[vmem] * 6,
        out_specs=(vmem, vmem, vmem),
        scratch_shapes=[
            pltpu.VMEM((GROUP, CHUNK, 2 * D), bf16),
            pltpu.VMEM((GROUP, CHUNK, 2 * D), bf16),
            pltpu.VMEM((NX, 2, D, SHARE), bf16),
            pltpu.VMEM((NX, 2, SHARE, D), bf16),
            pltpu.VMEM((NX, 2, D, SHARE), f32),
            pltpu.VMEM((ROWS, 2 * D), bf16),
            pltpu.VMEM((1, ROWS), i32),
            pltpu.VMEM((1, ROWS), i32),
            pltpu.VMEM((NX, CHUNK, SHARE), bf16),
            pltpu.VMEM((NX, CHUNK, SHARE), f32),
            pltpu.VMEM((NX, CHUNK, SHARE), bf16),
            pltpu.VMEM((D, D), f32),
            pltpu.VMEM((6, D, SHARE), bf16),
            pltpu.VMEM((6, D, SHARE), bf16),
            pltpu.VMEM((GROUP, 32, D), f32),
            pltpu.VMEM((NZ, 8, 128), f32),
            pltpu.VMEM((NZ, 8, 128), f32),
            pltpu.VMEM((NX, 8, 128), f32),
            pltpu.VMEM((NZ, 8, 128), f32),
            pltpu.VMEM((GROUP, NZ, 8, 128), f32),
            pltpu.VMEM((NZ, 1, CHUNK), f32),
            pltpu.VMEM((NZ, 1, CHUNK), f32),
            pltpu.VMEM((GROUP, NZ, 1, CHUNK), f32),
            dma((GROUP,)), dma((GROUP,)), pltpu.SemaphoreType.REGULAR,
            dma((6,)), dma((6,)),
            dma((6,)), dma((6,)),
            dma((7,)), dma((7,)),
        ],
        compiler_params=pltpu.CompilerParams(
            collective_id=0, has_side_effects=True, vmem_limit_bytes=56 << 20
        ),
        name="fused_step",
    )(
        cell_table,
        sample_index.reshape(1, ROWS),
        region.reshape(1, ROWS),
        targets,
        trunk_weight,
        expert_params[0],
    )
    new_params, new_first, new_second = adam_update(
        expert_params, first_moment, second_moment, grads[None]
    )
    return (trunk_grad, losses.reshape(ROWS), new_params, new_first, new_second)


def solution(mesh):
    placed = (
        P(("dp", "expert"), None),
        P(("dp", "expert")),
        P(("dp", "expert"), None),
        P(("dp", "expert"), None),
        P(),
        P("expert", None, None, "dp"),
        P("expert", None, None, "dp"),
        P("expert", None, None, "dp"),
    )
    return jax.shard_map(
        on_device,
        mesh=mesh,
        in_specs=placed,
        out_specs=(
            P(),
            P(("dp", "expert")),
            P("expert", None, None, "dp"),
            P("expert", None, None, "dp"),
            P("expert", None, None, "dp"),
        ),
        check_vma=False,
    )
```

time: 113 us -> 99.5 us (0.88)
  Pallas kernels: 108 us -> 93.7 us
    pallas_call x1, Pallas kernels: 108 us -> 93.7 us  [on_device(): pl.pallas_call(fused, out_shape=(jax.ShapeDtypeStruct((2, D, SHARE), f32)...]
where the time goes in v3:
time: 99.5 us; the launch traced here: 99.4 us
  Pallas kernels  93.7 us (94%)
  other arithmetic  3.71 us (4%)
  local copies, waits for them, and re-layouts  1.31 us (1%)
    pallas_call x1, Pallas kernels, on_device(): pl.pallas_call(fused, out_shape=(jax.ShapeDtypeStruct((2, D, SHARE), f32)...  93.7 us
    sub x1, other arithmetic, adam_update(): params - learn_rate * first_hat / (jnp.sqrt(second_hat) + adam_eps)  3.71 us

profile of v3, /device:TPU:1, one launch (start us, length us, event | category | flops | bytes accessed | tf_op | source)
XLA Modules:
  0.0 99.4 jit_solution(13468818518989546318)
XLA Ops:
  0.6 0.0 copy-start
  0.6 0.0 copy-start.1
  0.7 93.7 %fused_step.1 = (f32[2,256,512]{2,1,0:T(8,128)}, f32[1,1024]{1,0:T(1,128)}, f32[256,256]{1,0:T(8,128)}) custom-call(bf16[2048,256]{1,0:T(8,128)(2,1)} %table.1, s32[1,1024]{1,0:T(1,128)} %bitcast.13, s32[1,1024]{1,0:T(1,128)} %bitcast.14, bf16[1024,256]{1,0:T(8,128)(2,1)} %targets.1, bf16[256,256]{1,0:T(8,128)(2,1)} %wt.1, f32[2,256,512]{2,1,0:T(8,128)} %bitcast.12), custom_call_target="tpu_custom_call" | custom-call | tf_op jit(solution)/shard_map/fused_step/pallas_call | solution.py:363
  94.4 0.0 copy-done
  94.4 0.0 copy-done.1
  94.4 0.0 copy-start.2
  94.4 3.7 %divide_subtract_fusion = (f32[1,2,256,512]{3,2,1,0:T(8,128)}, f32[1,2,256,512]{3,2,1,0:T(8,128)}, f32[1,2,256,512]{3,2,1,0:T(8,128)}) fusion(f32[1,2,256,512]{3,2,1,0:T(8,128)S(1)} %copy-done, f32[2,256,512]{2,1,0:T(8,128)} %get-tuple-element.10, f32[1,2,256,512]{3,2,1,0:T(8,128)S(1)} %copy-done.1, f32[1,2,256,512]{3,2,1,0:T(8,128)} %param.15), kind=kLoop, calls=%fused_computation.4 | loop fusion | flops 3145728 | bytes 7340032 | tf_op jit(solution)/shard_map/sub | solution.py:37
  98.1 0.0 copy-done.2
  98.1 0.0 copy-start.3
  98.1 0.7 copy.15
  98.8 0.0 copy-done.3
  98.8 0.6 copy.16
Async XLA Ops:
  0.6 93.7 %copy-start = (f32[1,2,256,512]{3,2,1,0:T(8,128)S(1)}, f32[1,2,256,512]{3,2,1,0:T(8,128)}, u32[]{:S(2)}) copy-start(f32[1,2,256,512]{3,2,1,0:T(8,128)} %param.13) | copy-start | bytes 3145732
  0.6 93.7 %copy-start.1 = (f32[1,2,256,512]{3,2,1,0:T(8,128)S(1)}, f32[1,2,256,512]{3,2,1,0:T(8,128)}, u32[]{:S(2)}) copy-start(f32[1,2,256,512]{3,2,1,0:T(8,128)} %param.14) | copy-start | bytes 3145732
  94.4 3.7 %copy-start.2 = (f32[256,256]{1,0:T(8,128)S(1)}, f32[256,256]{1,0:T(8,128)}, u32[]{:S(2)}) copy-start(f32[256,256]{1,0:T(8,128)} %get-tuple-element.19) | copy-start | bytes 786436
  98.1 0.7 copy-start.3

commit v4 on v3

--- a/solution.py
+++ b/solution.py
@@ -202,9 +202,19 @@
     flip(2, 1)
 
     reduce = [
-        dp_copy(rs_s.at[n], rs_r.at[n], r_ss.at[n], r_rs.at[n], 1 if n in (0, 2, 4) else 3)
-        for n in range(6)
+        dp_copy(
+            rs_s.at[n, pl.ds(128 * h, 128)], rs_r.at[n, pl.ds(128 * h, 128)],
+            r_ss.at[n, h], r_rs.at[n, h], 1 if n in (0, 2, 4) else 3,
+        )
+        for n in range(6) for h in range(2)
     ]
+
+    def reduce_start(n, h):
+        reduce[2 * n + h].start()
+
+    def reduce_wait(n):
+        reduce[2 * n].wait_recv()
+        reduce[2 * n + 1].wait_recv()
     others = pl.ds(1, GROUP - 1)
     rest = pl.ds(CAP, CHUNK - CAP)
 
@@ -273,7 +283,9 @@
                 def _():
                     for n, m in {2: ((0, 0), (1, 1)), 1: ((2, 1),), 3: ((3, 0),)}[k]:
                         rs_s[n] = g[k, m].astype(bf16)
-                        reduce[n].start()
+                    if k == 2:
+                        for n, h in ((0, 0), (1, 0), (0, 1), (1, 1)):
+                            reduce_start(n, h)
 
     tr[0] = tacc[pl.ds(pl.multiple_of(mg * 32, 32), 32)]
     lmid[0] = lsend[0]
@@ -284,29 +296,34 @@
     for d in (4, 3, 5, 2, 6, 1, 7):
         plane_copy(tz.at[(mz + d) % NZ], zr.at[d], s_ss.at[2], s_rs.at[2], along_z(d)).start()
     zr[0] = tz[mz]
+    reduce_start(2, 0)
+    reduce_start(3, 0)
 
     plane_copy(lmid.at[others], lmid.at[others], s_ss.at[0], s_rs.at[0], me).wait_recv()
     for d in (4, 3, 5, 2, 6, 1, 7):
         plane_copy(lmid, lrecv.at[d], s_ss.at[3], s_rs.at[3], along_z(NZ - d)).start()
     lrecv[0] = lmid[...]
 
-    reduce[0].wait_recv()
+    reduce_wait(0)
     rs_s[4] = (g[1, 0] + rs_r[0].astype(f32)).astype(bf16)
-    reduce[4].start()
-    reduce[1].wait_recv()
+    reduce_wait(1)
     rs_s[5] = (g[3, 1] + rs_r[1].astype(f32)).astype(bf16)
-    reduce[5].start()
 
     plane_copy(zr.at[others], zr.at[others], s_ss.at[2], s_rs.at[2], me).wait_recv()
     xr[mx] = jnp.sum(zr[...], axis=0)
     for shift in (1, 2, 3):
         dp_copy(xr.at[mx], xr.at[mx], s_ss.at[4], s_rs.at[4], shift).start()
+
+    for n, h in ((2, 1), (3, 1), (4, 0), (5, 0)):
+        reduce_start(n, h)
 
     three = pl.ds(0, NX - 1)
     dp_copy(xr.at[three], xr.at[three], s_ss.at[4], s_rs.at[4], 1).wait_recv()
     agz[mz] = (xr[0] + xr[1]) + (xr[2] + xr[3])
     for d in (4, 3, 5, 2, 6, 1, 7):
         plane_copy(agz.at[mz], agz.at[mz], s_ss.at[5], s_rs.at[5], along_z(d)).start()
+    reduce_start(4, 1)
+    reduce_start(5, 1)
 
     plane_copy(lrecv.at[others], lrecv.at[others], s_ss.at[3], s_rs.at[3], me).wait_recv()
     table_f = lrecv[...].reshape(PLANE, CHUNK)
@@ -332,11 +349,11 @@
         plane_copy(agz, agb.at[mg], s_ss.at[6], s_rs.at[6], in_group(i)).start()
     agb[mg] = agz[...]
 
-    reduce[2].wait_recv()
-    reduce[3].wait_recv()
-    reduce[4].wait_recv()
+    reduce_wait(2)
+    reduce_wait(3)
+    reduce_wait(4)
     gout[0] = g[0, 0] + rs_r[3].astype(f32) + rs_r[4].astype(f32)
-    reduce[5].wait_recv()
+    reduce_wait(5)
     gout[1] = g[0, 1] + rs_r[2].astype(f32) + rs_r[5].astype(f32)
 
     plane_copy(agb.at[others], agb.at[others], s_ss.at[6], s_rs.at[6], me).wait_recv()
@@ -395,7 +412,7 @@
             pltpu.VMEM((GROUP, NZ, 1, CHUNK), f32),
             dma((GROUP,)), dma((GROUP,)), pltpu.SemaphoreType.REGULAR,
             dma((6,)), dma((6,)),
-            dma((6,)), dma((6,)),
+            dma((6, 2)), dma((6, 2)),
             dma((7,)), dma((7,)),
         ],
         compiler_params=pltpu.CompilerParams(

time: 99.5 us -> 92.3 us (0.928)
  Pallas kernels: 93.7 us -> 86.5 us
    pallas_call x1, Pallas kernels: 93.7 us -> 86.5 us  [on_device(): pl.pallas_call(fused, out_shape=(jax.ShapeDtypeStruct((2, D, SHARE), f32)...]
where the time goes in v4:
time: 92.3 us; the launch traced here: 92.2 us
  Pallas kernels  86.5 us (94%)
  other arithmetic  3.71 us (4%)
  local copies, waits for them, and re-layouts  1.31 us (1%)
    pallas_call x1, Pallas kernels, on_device(): pl.pallas_call(fused, out_shape=(jax.ShapeDtypeStruct((2, D, SHARE), f32)...  86.5 us
    sub x1, other arithmetic, adam_update(): params - learn_rate * first_hat / (jnp.sqrt(second_hat) + adam_eps)  3.71 us

profile of v4, /device:TPU:1, one launch (start us, length us, event | category | flops | bytes accessed | tf_op | source)
XLA Modules:
  0.0 92.2 jit_solution(16809370902373371963)
XLA Ops:
  0.6 0.0 copy-start
  0.6 0.0 copy-start.1
  0.7 86.5 %fused_step.1 = (f32[2,256,512]{2,1,0:T(8,128)}, f32[1,1024]{1,0:T(1,128)}, f32[256,256]{1,0:T(8,128)}) custom-call(bf16[2048,256]{1,0:T(8,128)(2,1)} %table.1, s32[1,1024]{1,0:T(1,128)} %bitcast.13, s32[1,1024]{1,0:T(1,128)} %bitcast.14, bf16[1024,256]{1,0:T(8,128)(2,1)} %targets.1, bf16[256,256]{1,0:T(8,128)(2,1)} %wt.1, f32[2,256,512]{2,1,0:T(8,128)} %bitcast.12), custom_call_target="tpu_custom_call" | custom-call | tf_op jit(solution)/shard_map/fused_step/pallas_call | solution.py:380
  87.1 0.0 copy-done
  87.1 0.0 copy-done.1
  87.1 0.0 copy-start.2
  87.2 3.7 %divide_subtract_fusion = (f32[1,2,256,512]{3,2,1,0:T(8,128)}, f32[1,2,256,512]{3,2,1,0:T(8,128)}, f32[1,2,256,512]{3,2,1,0:T(8,128)}) fusion(f32[1,2,256,512]{3,2,1,0:T(8,128)S(1)} %copy-done, f32[2,256,512]{2,1,0:T(8,128)} %get-tuple-element.10, f32[1,2,256,512]{3,2,1,0:T(8,128)S(1)} %copy-done.1, f32[1,2,256,512]{3,2,1,0:T(8,128)} %param.15), kind=kLoop, calls=%fused_computation.4 | loop fusion | flops 3145728 | bytes 7340032 | tf_op jit(solution)/shard_map/sub | solution.py:37
  90.9 0.0 copy-done.2
  90.9 0.0 copy-start.3
  90.9 0.7 copy.15
  91.6 0.0 copy-done.3
  91.6 0.6 copy.16
Async XLA Ops:
  0.6 86.5 %copy-start = (f32[1,2,256,512]{3,2,1,0:T(8,128)S(1)}, f32[1,2,256,512]{3,2,1,0:T(8,128)}, u32[]{:S(2)}) copy-start(f32[1,2,256,512]{3,2,1,0:T(8,128)} %param.13) | copy-start | bytes 3145732
  0.6 86.5 %copy-start.1 = (f32[1,2,256,512]{3,2,1,0:T(8,128)S(1)}, f32[1,2,256,512]{3,2,1,0:T(8,128)}, u32[]{:S(2)}) copy-start(f32[1,2,256,512]{3,2,1,0:T(8,128)} %param.14) | copy-start | bytes 3145732
  87.1 3.7 %copy-start.2 = (f32[256,256]{1,0:T(8,128)S(1)}, f32[256,256]{1,0:T(8,128)}, u32[]{:S(2)}) copy-start(f32[256,256]{1,0:T(8,128)} %get-tuple-element.19) | copy-start | bytes 786436
  90.9 0.7 copy-start.3

commit v5 on v4

--- a/solution.py
+++ b/solution.py
@@ -26,6 +26,13 @@
 CAP = 32
 CHUNK = GROUP * CAP
 SHARE = 512
+HALF = CHUNK
+POS = (3, 6, 4, 1, 0, 2, 5, 7)
+FAR = (4, 3, 5, 0, 2, 6, 1, 7)
+
+
+def order_of(t):
+    return t
 
 
 def adam_update(params, first, second, grads):
@@ -53,9 +60,9 @@
 
 
 def fused(
-    table, sidx, region, targets, wt, params,
+    table_in, sidx_in, region_in, targets_in, wt_in, params_in,
     gout, loss_out, tg_out,
-    send, recv, w, wt_t, g, pay, qrow, place, hbuf, sbuf, pbuf, tacc,
+    table, params, sidx, region, wt, in_sem, send, recv, w, wt_t, g, pay, qrow, place, hbuf, sbuf, pbuf, tacc,
     rs_s, rs_r, tr, tz, zr, xr, agz, agb, lsend, lmid, lrecv,
     a_ss, a_rs, ready, ag_ss, ag_rs, r_ss, r_rs, s_ss, s_rs,
 ):
@@ -90,6 +97,17 @@
             device_id={"dp": (mx + shift) % NX}, device_id_type=MESH,
         )
 
+    loads = [
+        pltpu.make_async_copy(params_in, params, in_sem.at[0]),
+        pltpu.make_async_copy(table_in, table, in_sem.at[1]),
+        pltpu.make_async_copy(targets_in, pay.at[:, pl.ds(D, D)], in_sem.at[2]),
+        pltpu.make_async_copy(region_in, region, in_sem.at[3]),
+        pltpu.make_async_copy(sidx_in, sidx, in_sem.at[4]),
+        pltpu.make_async_copy(wt_in, wt, in_sem.at[5]),
+    ]
+    for n in (3, 4, 1, 2, 0, 5):
+        loads[n].start()
+
     barrier = pltpu.get_barrier_semaphore()
     for d in (4, 3, 5, 2, 6, 1, 7):
         pl.semaphore_signal(barrier, inc=1, device_id={"expert": along_z(d)}, device_id_type=MESH)
@@ -100,8 +118,7 @@
             barrier, inc=1, device_id={"dp": (mx + shift) % NX}, device_id_type=MESH
         )
 
-    w[0] = params[...].astype(bf16)
-
+    loads[3].wait()
     named = region[...]
     q = (
         ((((named >> 1) & (NY - 1)) - my) & (NY - 1)) * NC * NZ
@@ -109,6 +126,8 @@
         + (((named >> 3) - mz) & (NZ - 1))
     )
     qrow[...] = q
+    along = q & (NZ - 1)
+    spread = q - along + sum(jnp.where(along == d, POS[d], 0) for d in range(NZ))
     before = onehot(
         lax.broadcasted_iota(i32, (256, 256), 0) < lax.broadcasted_iota(i32, (256, 256), 1)
     )
@@ -119,8 +138,10 @@
         count = dot(hot.astype(bf16), before) + carry
         slot = jnp.sum(hot * count, axis=0, keepdims=True)
         carry = carry + jnp.sum(hot, axis=1, keepdims=True)
-        place[:, 256 * b : 256 * b + 256] = part * CAP + slot.astype(i32)
-
+        place[:, 256 * b : 256 * b + 256] = spread[:, 256 * b : 256 * b + 256] * CAP + slot.astype(i32)
+
+    loads[1].wait()
+    loads[4].wait()
     for b in range(ROWS // 256):
         cols = [
             jnp.transpose(
@@ -134,23 +155,29 @@
         wide = jnp.concatenate([col] * (CELLS // 128), axis=1)
         pick = onehot(wide == lax.broadcasted_iota(i32, (256, CELLS), 1))
         pay[256 * b : 256 * b + 256, :D] = dot(pick, table[...]).astype(bf16)
-    pay[:, D:] = targets[...]
+    loads[2].wait()
 
     def pack(i):
         mask = lax.broadcasted_iota(i32, (CHUNK, ROWS), 0) + i * CHUNK == place[...]
         send[i] = dot(onehot(mask), pay[...]).astype(bf16)
 
     def row_copy(i, d):
-        rows = pl.ds(d * CAP, CAP)
+        rows = pl.ds(POS[d] * CAP, CAP)
+        h = POS[d] * CAP // HALF
         return plane_copy(
-            send.at[i, rows], recv.at[i, rows], a_ss.at[i], a_rs.at[i], owner(i, d)
+            send.at[i, rows], recv.at[i, rows], a_ss.at[i, h], a_rs.at[i, h], owner(i, d)
         )
 
     pack(0)
-    recv[0, 0:CAP] = send[0, 0:CAP]
+    own = POS[0] * CAP
+    recv[0, own : own + CAP] = send[0, own : own + CAP]
+    loads[0].wait()
+    loads[5].wait()
+    w[0] = params[...].astype(bf16)
     pl.semaphore_wait(barrier, NZ - 1 + GROUP - 1 + NX - 1)
-    for d in (4, 3, 5, 2, 6, 1, 7):
-        row_copy(0, d).start()
+    for d in FAR:
+        if d:
+            row_copy(0, d).start()
 
     for i in range(1, GROUP):
         pl.semaphore_signal(ready, inc=1, device_id={"expert": in_group(i)}, device_id_type=MESH)
@@ -166,17 +193,17 @@
     for copy in gather[:4]:
         copy.start()
 
-    pack(1)
+    pack(order_of(1))
     pl.semaphore_wait(ready, GROUP - 1)
 
     @pl.loop(1, GROUP)
-    def _(i):
-        for d in (4, 3, 5, 2, 6, 1, 7, 0):
-            row_copy(i, d).start()
-
-        @pl.when(i < GROUP - 1)
+    def _(t):
+        for d in FAR:
+            row_copy(order_of(t), d).start()
+
+        @pl.when(t < GROUP - 1)
         def _():
-            pack(i + 1)
+            pack(order_of(t + 1))
 
     g[...] = jnp.zeros_like(g)
     tacc[...] = jnp.zeros_like(tacc)
@@ -216,26 +243,33 @@
         reduce[2 * n].wait_recv()
         reduce[2 * n + 1].wait_recv()
     others = pl.ds(1, GROUP - 1)
-    rest = pl.ds(CAP, CHUNK - CAP)
+
+    def half(ref_a, ref_b, i, h, first):
+        rows = pl.ds(h * HALF if isinstance(h, int) else pl.multiple_of(h * HALF, HALF), HALF - CAP if first else HALF)
+        return plane_copy(ref_a.at[i, rows], ref_b.at[i, rows], a_ss.at[i, h], a_rs.at[i, h], me)
 
     @pl.loop(0, GROUP)
     def _(t):
+        i = order_of(t)
+        h = 0
+
         @pl.when(t == 0)
         def _():
-            plane_copy(send.at[0, rest], recv.at[0, rest], a_ss.at[0], a_rs.at[0], me).wait_recv()
+            half(send, recv, 0, 0, True).wait_recv()
 
         @pl.when(t != 0)
         def _():
-            plane_copy(send.at[t], recv.at[t], a_ss.at[t], a_rs.at[t], me).wait_recv()
-
-        feats = recv[t, :, :D]
+            half(send, recv, i, h, False).wait_recv()
+
+        rows = pl.ds(pl.multiple_of(h * HALF, HALF), HALF)
+        feats = recv[i, rows, :D]
         feats_f = feats.astype(f32)
         trunk_pre = dot(feats, wt[...])
         trunk_sig = sigmoid(trunk_pre)
         trunk_f = feats_f + trunk_pre * trunk_sig
         trunk_out = trunk_f.astype(bf16)
         trunk_t = jnp.transpose(trunk_f).astype(bf16)
-        predicted = jnp.zeros((CHUNK, D), f32)
+        predicted = jnp.zeros((HALF, D), f32)
         for k in range(NX):
             up = dot(trunk_out, w[k, 0])
             sig = sigmoid(up)
@@ -244,21 +278,21 @@
             hbuf[k] = hid_b
             sbuf[k] = sig + hid * (1.0 - sig)
             predicted = predicted + dot(hid_b, wt_t[k, 1])
-        errors = predicted - recv[t, :, D:].astype(f32)
+        errors = predicted - recv[i, rows, D:].astype(f32)
         squares = errors * errors
         squares = jnp.transpose(squares[:, :128] + squares[:, 128:])
-        lsend[t] = jnp.sum(squares, axis=0, keepdims=True) * (0.5 * loss_scale)
-
-        @pl.when(t != 0)
+        lsend[i, h] = jnp.sum(squares, axis=0, keepdims=True) * (0.5 * loss_scale)
+
+        @pl.when(i != 0)
         def _():
             plane_copy(
-                lsend.at[t], lmid.at[t], s_ss.at[0], s_rs.at[0], before_in_group(t)
+                lsend.at[i], lmid.at[i], s_ss.at[0], s_rs.at[0], before_in_group(i)
             ).start()
 
         scaled_f = errors * loss_scale
         scaled = scaled_f.astype(bf16)
         scaled_t = jnp.transpose(scaled_f).astype(bf16)
-        row_grad = jnp.zeros((CHUNK, D), f32)
+        row_grad = jnp.zeros((HALF, D), f32)
         for k in range(NX):
             pre_grad = (dot(scaled, w[k, 1]) * sbuf[k]).astype(bf16)
             pbuf[k] = pre_grad
@@ -326,7 +360,9 @@
     reduce_start(5, 1)
 
     plane_copy(lrecv.at[others], lrecv.at[others], s_ss.at[3], s_rs.at[3], me).wait_recv()
-    table_f = lrecv[...].reshape(PLANE, CHUNK)
+    table_f = jnp.concatenate(
+        [lrecv[:, :, h].reshape(PLANE, HALF) for h in range(CHUNK // HALF)], axis=1
+    )
     high = table_f.astype(bf16)
     left = table_f - high.astype(f32)
     middle = left.astype(bf16)
@@ -362,9 +398,9 @@
             row, col = 32 * i + 8 * (p % 4), 128 * (p // 4)
             tg_out[row : row + 8, col : col + 128] = agb[i, p]
 
-    plane_copy(send.at[0, rest], recv.at[0, rest], a_ss.at[0], a_rs.at[0], me).wait_send()
-    for i in range(1, GROUP):
-        plane_copy(send.at[i], recv.at[i], a_ss.at[i], a_rs.at[i], me).wait_send()
+    for i in range(GROUP):
+        for h in range(CHUNK // HALF):
+            half(send, recv, i, h, i == 0 and h == 0).wait_send()
     for copy in gather + reduce:
         copy.wait_send()
     for n, ref in ((0, lmid), (1, tr), (2, zr), (3, lrecv), (5, agz), (6, agb)):
@@ -376,6 +412,7 @@
     cell_table, sample_index, region, targets, trunk_weight, expert_params, first_moment, second_moment
 ):
     vmem = pl.BlockSpec(memory_space=pltpu.VMEM)
+    hbm = pl.BlockSpec(memory_space=pltpu.HBM)
     dma = pltpu.SemaphoreType.DMA
     grads, losses, trunk_grad = pl.pallas_call(
         fused,
@@ -384,9 +421,15 @@
             jax.ShapeDtypeStruct((1, ROWS), f32),
             jax.ShapeDtypeStruct((D, D), f32),
         ),
-        in_specs=[vmem] * 6,
+        in_specs=[hbm] * 6,
         out_specs=(vmem, vmem, vmem),
         scratch_shapes=[
+            pltpu.VMEM((CELLS, D), bf16),
+            pltpu.VMEM((2, D, SHARE), f32),
+            pltpu.VMEM((1, ROWS), i32),
+            pltpu.VMEM((1, ROWS), i32),
+            pltpu.VMEM((D, D), bf16),
+            dma((6,)),
             pltpu.VMEM((GROUP, CHUNK, 2 * D), bf16),
             pltpu.VMEM((GROUP, CHUNK, 2 * D), bf16),
             pltpu.VMEM((NX, 2, D, SHARE), bf16),
@@ -395,9 +438,9 @@
             pltpu.VMEM((ROWS, 2 * D), bf16),
             pltpu.VMEM((1, ROWS), i32),
             pltpu.VMEM((1, ROWS), i32),
-            pltpu.VMEM((NX, CHUNK, SHARE), bf16),
-            pltpu.VMEM((NX, CHUNK, SHARE), f32),
-            pltpu.VMEM((NX, CHUNK, SHARE), bf16),
+            pltpu.VMEM((NX, HALF, SHARE), bf16),
+            pltpu.VMEM((NX, HALF, SHARE), f32),
+            pltpu.VMEM((NX, HALF, SHARE), bf16),
             pltpu.VMEM((D, D), f32),
             pltpu.VMEM((6, D, SHARE), bf16),
             pltpu.VMEM((6, D, SHARE), bf16),
@@ -407,25 +450,30 @@
             pltpu.VMEM((NX, 8, 128), f32),
             pltpu.VMEM((NZ, 8, 128), f32),
             pltpu.VMEM((GROUP, NZ, 8, 128), f32),
-            pltpu.VMEM((NZ, 1, CHUNK), f32),
-            pltpu.VMEM((NZ, 1, CHUNK), f32),
-            pltpu.VMEM((GROUP, NZ, 1, CHUNK), f32),
-            dma((GROUP,)), dma((GROUP,)), pltpu.SemaphoreType.REGULAR,
+            pltpu.VMEM((GROUP, 1, 1, HALF), f32),
+            pltpu.VMEM((GROUP, 1, 1, HALF), f32),
+            pltpu.VMEM((NZ, GROUP, 1, 1, HALF), f32),
+            dma((GROUP, 1)), dma((GROUP, 1)), pltpu.SemaphoreType.REGULAR,
             dma((6,)), dma((6,)),
             dma((6, 2)), dma((6, 2)),
             dma((7,)), dma((7,)),
         ],
         compiler_params=pltpu.CompilerParams(
-            collective_id=0, has_side_effects=True, vmem_limit_bytes=56 << 20
+            collective_id=0, has_side_effects=True, vmem_limit_bytes=36 << 20
         ),
         name="fused_step",
     )(
-        cell_table,
-        sample_index.reshape(1, ROWS),
-        region.reshape(1, ROWS),
-        targets,
-        trunk_weight,
-        expert_params[0],
+        *(
+            pltpu.with_memory_space_constraint(value, pltpu.HBM)
+            for value in (
+                cell_table,
+                sample_index.reshape(1, ROWS),
+                region.reshape(1, ROWS),
+                targets,
+                trunk_weight,
+                expert_params[0],
+            )
+        )
     )
     new_params, new_first, new_second = adam_update(
         expert_params, first_moment, second_moment, grads[None]

time: 92.3 us -> 89.3 us (0.967)
  Pallas kernels: 86.5 us -> 83.8 us
    pallas_call x1, Pallas kernels: 86.5 us -> 83.8 us  [on_device(): pl.pallas_call(fused, out_shape=(jax.ShapeDtypeStruct((2, D, SHARE), f32)...]
where the time goes in v5:
time: 89.3 us; the launch traced here: 89.2 us
  Pallas kernels  83.8 us (94%)
  other arithmetic  3.38 us (4%)
  local copies, waits for them, and re-layouts  1.3 us (1%)
    pallas_call x1, Pallas kernels, on_device(): pl.pallas_call(fused, out_shape=(jax.ShapeDtypeStruct((2, D, SHARE), f32)...  83.8 us
    sub x1, other arithmetic, adam_update(): params - learn_rate * first_hat / (jnp.sqrt(second_hat) + adam_eps)  3.38 us

profile of v5, /device:TPU:1, one launch (start us, length us, event | category | flops | bytes accessed | tf_op | source)
XLA Modules:
  0.0 89.2 jit_solution(15956583992453207660)
XLA Ops:
  0.6 0.0 copy-start
  0.6 0.0 copy-start.1
  0.7 83.8 %fused_step.1 = (f32[2,256,512]{2,1,0:T(8,128)S(1)}, f32[1,1024]{1,0:T(1,128)S(1)}, f32[256,256]{1,0:T(8,128)S(1)}) custom-call(bf16[2048,256]{1,0:T(8,128)(2,1)} %table_in.1, s32[1,1024]{1,0:T(1,128)} %bitcast.14, s32[1,1024]{1,0:T(1,128)} %bitcast.15, bf16[1024,256]{1,0:T(8,128)(2,1)} %targets_in.1, bf16[256,256]{1,0:T(8,128)(2,1)} %wt_in.1, ...), custom_call_target="tpu_custom_call" | custom-call | tf_op jit(solution)/shard_map/fused_step/pallas_call | solution.py:417
  84.5 0.0 copy-done
  84.5 0.0 copy-done.1
  84.5 3.4 %divide_subtract_fusion = (f32[1,2,256,512]{3,2,1,0:T(8,128)}, f32[1,2,256,512]{3,2,1,0:T(8,128)}, f32[1,2,256,512]{3,2,1,0:T(8,128)}) fusion(f32[1,2,256,512]{3,2,1,0:T(8,128)S(1)} %copy-done, f32[2,256,512]{2,1,0:T(8,128)S(1)} %get-tuple-element.10, f32[1,2,256,512]{3,2,1,0:T(8,128)S(1)} %copy-done.1, f32[1,2,256,512]{3,2,1,0:T(8,128)} %param.15), kind=kLoop, calls=%fused_computation.4 | loop fusion | flops 3145728 | bytes 7340032 | tf_op jit(solution)/shard_map/sub | solution.py:44
  87.9 0.7 copy.15
  88.6 0.6 copy.16
Async XLA Ops:
  0.6 83.9 %copy-start = (f32[1,2,256,512]{3,2,1,0:T(8,128)S(1)}, f32[1,2,256,512]{3,2,1,0:T(8,128)}, u32[]{:S(2)}) copy-start(f32[1,2,256,512]{3,2,1,0:T(8,128)} %param.13) | copy-start | bytes 3145732
  0.6 83.9 %copy-start.1 = (f32[1,2,256,512]{3,2,1,0:T(8,128)S(1)}, f32[1,2,256,512]{3,2,1,0:T(8,128)}, u32[]{:S(2)}) copy-start(f32[1,2,256,512]{3,2,1,0:T(8,128)} %param.14) | copy-start | bytes 3145732

commit v6 on v5

--- a/solution.py
+++ b/solution.py
@@ -38,13 +38,9 @@
 def adam_update(params, first, second, grads):
     first_new = beta_one * first + (1.0 - beta_one) * grads
     second_new = beta_two * second + (1.0 - beta_two) * grads * grads
-    first_hat = first_new / (1.0 - beta_one**adam_step)
-    second_hat = second_new / (1.0 - beta_two**adam_step)
-    return (
-        params - learn_rate * first_hat / (jnp.sqrt(second_hat) + adam_eps),
-        first_new,
-        second_new,
-    )
+    root = jnp.sqrt(second_new * (1.0 / (1.0 - beta_two**adam_step)))
+    step = first_new * (learn_rate / (1.0 - beta_one**adam_step))
+    return (params - step / (root + adam_eps), first_new, second_new)
 
 
 def dot(a, b):
@@ -348,16 +344,16 @@
     for shift in (1, 2, 3):
         dp_copy(xr.at[mx], xr.at[mx], s_ss.at[4], s_rs.at[4], shift).start()
 
-    for n, h in ((2, 1), (3, 1), (4, 0), (5, 0)):
-        reduce_start(n, h)
+    reduce_start(2, 1)
+    reduce_start(3, 1)
 
     three = pl.ds(0, NX - 1)
     dp_copy(xr.at[three], xr.at[three], s_ss.at[4], s_rs.at[4], 1).wait_recv()
     agz[mz] = (xr[0] + xr[1]) + (xr[2] + xr[3])
     for d in (4, 3, 5, 2, 6, 1, 7):
         plane_copy(agz.at[mz], agz.at[mz], s_ss.at[5], s_rs.at[5], along_z(d)).start()
-    reduce_start(4, 1)
-    reduce_start(5, 1)
+    for n, h in ((4, 0), (5, 0), (4, 1), (5, 1)):
+        reduce_start(n, h)
 
     plane_copy(lrecv.at[others], lrecv.at[others], s_ss.at[3], s_rs.at[3], me).wait_recv()
     table_f = jnp.concatenate(

time: 89.3 us -> 89.3 us (level)
  no operation moved by 1% of the time
where the time goes in v6:
time: 89.3 us; the launch traced here: 89.2 us
  Pallas kernels  83.8 us (94%)
  other arithmetic  3.38 us (4%)
  local copies, waits for them, and re-layouts  1.3 us (1%)
    pallas_call x1, Pallas kernels, on_device(): pl.pallas_call(fused, out_shape=(jax.ShapeDtypeStruct((2, D, SHARE), f32)...  83.8 us
    sub x1, other arithmetic, adam_update(): return (params - step / (root + adam_eps), first_new, second_new)  3.38 us

profile of v6, /device:TPU:1, one launch (start us, length us, event | category | flops | bytes accessed | tf_op | source)
XLA Modules:
  0.0 89.2 jit_solution(16352920086698870380)
XLA Ops:
  0.6 0.0 copy-start
  0.6 0.0 copy-start.1
  0.7 83.8 %fused_step.1 = (f32[2,256,512]{2,1,0:T(8,128)S(1)}, f32[1,1024]{1,0:T(1,128)S(1)}, f32[256,256]{1,0:T(8,128)S(1)}) custom-call(bf16[2048,256]{1,0:T(8,128)(2,1)} %table_in.1, s32[1,1024]{1,0:T(1,128)} %bitcast.14, s32[1,1024]{1,0:T(1,128)} %bitcast.15, bf16[1024,256]{1,0:T(8,128)(2,1)} %targets_in.1, bf16[256,256]{1,0:T(8,128)(2,1)} %wt_in.1, ...), custom_call_target="tpu_custom_call" | custom-call | tf_op jit(solution)/shard_map/fused_step/pallas_call | solution.py:413
  84.5 0.0 copy-done
  84.5 0.0 copy-done.1
  84.5 3.4 %divide_subtract_fusion = (f32[1,2,256,512]{3,2,1,0:T(8,128)}, f32[1,2,256,512]{3,2,1,0:T(8,128)}, f32[1,2,256,512]{3,2,1,0:T(8,128)}) fusion(f32[1,2,256,512]{3,2,1,0:T(8,128)S(1)} %copy-done, f32[2,256,512]{2,1,0:T(8,128)S(1)} %get-tuple-element.10, f32[1,2,256,512]{3,2,1,0:T(8,128)S(1)} %copy-done.1, f32[1,2,256,512]{3,2,1,0:T(8,128)} %param.15), kind=kLoop, calls=%fused_computation.4 | loop fusion | flops 3145728 | bytes 7340032 | tf_op jit(solution)/shard_map/sub | solution.py:43
  87.9 0.7 copy.15
  88.6 0.6 copy.16
Async XLA Ops:
  0.6 83.9 %copy-start = (f32[1,2,256,512]{3,2,1,0:T(8,128)S(1)}, f32[1,2,256,512]{3,2,1,0:T(8,128)}, u32[]{:S(2)}) copy-start(f32[1,2,256,512]{3,2,1,0:T(8,128)} %param.13) | copy-start | bytes 3145732
  0.6 83.9 %copy-start.1 = (f32[1,2,256,512]{3,2,1,0:T(8,128)S(1)}, f32[1,2,256,512]{3,2,1,0:T(8,128)}, u32[]{:S(2)}) copy-start(f32[1,2,256,512]{3,2,1,0:T(8,128)} %param.14) | copy-start | bytes 3145732
